TPU v7x, 128 devices: a whole 4x4x4 slice. The times are simulated.
128 devices in a mesh: replica: 8 (over x, y_hi), shard: 16 (over z, y_lo, core).
Axes of the slice: x: 4, y: 4 (y_hi: 2, y_lo: 2; y = y_hi * 2 + y_lo), z: 4, core: 2. Of those that a mesh axis runs over, the one named last changes fastest.
Arguments:
- tokens: bfloat16 [65536, 1920], P(('replica', 'shard')), may hold values from -36 to 36
- timesteps: int32 [256], P(('replica', 'shard')), may hold values from 0 to 63
- table: float32 [64, 2, 1920], replicated, may hold values from -3 to 3
- weight_values: bfloat16 [4864, 1920], P('shard'), may hold values from -0.125 to 0.125
- weight_scales: bfloat16 [4864, 15], P('shard'), may hold values from 0.29882812 to 3
- cotangent: bfloat16 [65536, 4864], P(('replica', 'shard')), may hold values from -24 to 24
Outputs:
- hidden: bfloat16 [65536, 4864], P(('replica', 'shard'))
- grad_weight: float32 [4864, 1920], P('shard')
- grad_tokens: bfloat16 [65536, 1920], P(('replica', 'shard'))
All inputs are finite; a program needn't handle non-finite values.
Results may differ from a plain program's by a relative error of at most 0.02.
Values may be sent and summed in bfloat16 or wider, within the bound.
A program may use at most 256 MiB of HBM per device.

v0:
```python
import jax
import jax.numpy as jnp
from jax import lax
from jax.sharding import PartitionSpec as P

root_two_over_pi = 0.7978845608028654
cubic_coef = 0.044715
epsilon = 1e-06


def gelu_slope(preact):
    inner_term = root_two_over_pi * (preact + cubic_coef * preact * preact * preact)
    tangent = jnp.tanh(inner_term)
    gelu_value = 0.5 * preact * (1.0 + tangent)
    derivative = 0.5 * (1.0 + tangent) + 0.5 * preact * (
        1.0 - tangent * tangent
    ) * root_two_over_pi * (1.0 + 3.0 * cubic_coef * preact * preact)
    return (gelu_value, derivative)


def dequantize(weight_values, weight_scales):
    row_count, features = weight_values.shape
    blocks = weight_scales.shape[1]
    expanded = (
        weight_values.astype(jnp.float32).reshape(row_count, blocks, features // blocks)
        * weight_scales.astype(jnp.float32)[:, :, None]
    )
    return expanded.reshape(row_count, features).astype(jnp.bfloat16)


def modulate(tokens, timesteps, table):
    samples = timesteps.shape[0]
    step_count = table.shape[0]
    features = tokens.shape[1]
    onehot = (timesteps[:, None] == jnp.arange(step_count, dtype=jnp.int32)[None, :]).astype(
        jnp.float32
    )
    picked = jnp.dot(
        onehot, table.reshape(step_count, 2 * features), precision=lax.Precision.HIGHEST
    )
    picked = picked.reshape(samples, 2, features)
    grouped = tokens.astype(jnp.float32).reshape(samples, -1, features)
    centre = grouped - jnp.mean(grouped, axis=2, keepdims=True)
    inverse = lax.rsqrt(jnp.mean(centre * centre, axis=2, keepdims=True) + epsilon)
    normed = centre * inverse
    factor = 1.0 + picked[:, 1][:, None, :]
    moved = (normed * factor + picked[:, 0][:, None, :]).reshape(-1, features).astype(jnp.bfloat16)
    return (moved, normed, inverse, factor)


def normalize_back(grad_moved, normed, inverse, factor):
    samples = normed.shape[0]
    features = normed.shape[2]
    scaled_grad = grad_moved.reshape(samples, -1, features) * factor
    mean_grad = jnp.mean(scaled_grad, axis=2, keepdims=True)
    mean_prod = jnp.mean(scaled_grad * normed, axis=2, keepdims=True)
    result = inverse * (scaled_grad - mean_grad - normed * mean_prod)
    return result.reshape(-1, features).astype(jnp.bfloat16)


def per_device(tokens, timesteps, table, weight_values, weight_scales, cotangent):
    moved, normed, inverse, factor = modulate(tokens, timesteps, table)
    upstream = cotangent.astype(jnp.float32)
    gathered_values, gathered_scales = (
        lax.all_gather(weight_values, "shard", axis=0, tiled=True),
        lax.all_gather(weight_scales, "shard", axis=0, tiled=True),
    )
    weight = dequantize(gathered_values, gathered_scales)
    preact = jnp.einsum("td,fd->tf", moved, weight, preferred_element_type=jnp.float32)
    gelu_value, derivative = gelu_slope(preact)
    hidden = gelu_value.astype(jnp.bfloat16)
    grad_pre = (upstream * derivative).astype(jnp.bfloat16)
    grad_moved = jnp.dot(grad_pre, weight, preferred_element_type=jnp.float32)
    product = lax.dot_general(
        grad_pre, moved, (((0,), (0,)), ((), ())), preferred_element_type=jnp.float32
    )
    rounded = lax.optimization_barrier(product.astype(jnp.bfloat16))
    group_part = lax.psum_scatter(
        rounded.astype(jnp.float32).astype(jnp.bfloat16), "shard", scatter_dimension=0, tiled=True
    )
    grad_weight = lax.psum(group_part, "replica").astype(jnp.float32)
    grad_tokens = normalize_back(grad_moved, normed, inverse, factor)
    return (hidden, grad_weight, grad_tokens)


def solution(mesh):
    placed = (
        P(("replica", "shard"), None),
        P(("replica", "shard")),
        P(),
        P("shard", None),
        P("shard", None),
        P(("replica", "shard"), None),
    )
    return jax.shard_map(
        per_device,
        mesh=mesh,
        in_specs=placed,
        out_specs=(P(("replica", "shard"), None), P("shard", None), P(("replica", "shard"), None)),
        check_vma=False,
    )
```

profile of v0, /device:TPU:0, one launch (start us, length us, event | category | flops | bytes accessed | tf_op | source)
XLA Modules:
  0.0 496.3 jit_solution(2334483835488481920)
XLA Ops:
  7.2 0.0 copy-start
  7.2 0.0 copy-start.3
  7.2 0.0 all-gather.3.cloned.1.call-start
  7.2 0.7 all-gather.3.cloned.1.call-update
  7.9 0.0 reduce-scatter.2.cloned.1.call-start
  8.0 22.6 %all-gather = bf16[16,304,15]{1,2,0:T(8,128)(2,1)S(1)} all-gather(bf16[1,304,15]{1,2,0:T(8,128)(2,1)} %bitcast.51), channel_id=1, replica_groups=mesh['replica'=8,'shard'=16] {'shard'}, dimensions={0}, use_global_device_ids=true | all-gather | bytes 155040 | tf_op jit(solution)/shard_map/all_gather | solution.py:66
  30.7 0.2 reshape.71
  30.9 0.0 copy-done
  30.9 0.0 copy-start.2
  30.9 0.3 convert_reduce_fusion
  31.3 0.7 multiply_reduce_fusion.1
  31.9 0.0 copy-done.3
  31.9 0.2 copy-done.2
  32.1 0.4 fusion.11
  32.6 2.5 fusion.10
  35.1 77.8 %all-gather.3.cloned.1.call-done = bf16[4864,1920]{1,0:T(8,128)(2,1)} async-done(((bf16[304,1920]{1,0:T(8,128)(2,1)}), bf16[4864,1920]{1,0:T(8,128)(2,1)}) %all-gather.3.cloned.1.call-update) | async-done | bytes 18677776 | tf_op jit(solution)/shard_map/all_gather | solution.py:65
  112.8 23.3 %copy.18 = bf16[4864,1920]{0,1:T(8,128)(2,1)} copy(bf16[4864,1920]{1,0:T(8,128)(2,1)} %all-gather.3.cloned.1.call-done) | data formatting | bytes 37355520 | tf_op jit(solution)/shard_map/all_gather | solution.py:65
  136.2 0.0 copy-start.1
  136.2 17.3 %fusion = bf16[4864,1920]{0,1:T(8,128)(2,1)} fusion(bf16[4864,1920]{0,1:T(8,128)(2,1)} %copy.18, f32[4864,15]{0,1:T(8,128)S(1)} %reshape.71), kind=kLoop, calls=%fused_computation.1 | loop fusion | flops 28016640 | bytes 37647360 | tf_op jit(solution)/shard_map/convert_element_type | solution.py:28
  153.5 0.0 copy-done.1
  153.5 21.5 %fusion.9 = (bf16[512,4864]{1,0:T(8,128)(2,1)S(1)}, bf16[512,4864]{1,0:T(8,128)(2,1)}) fusion(bf16[512,4864]{1,0:T(8,128)(2,1)} %param.11, bf16[512,1920]{1,0:T(8,128)(2,1)S(1)} %copy-done.1, bf16[4864,1920]{0,1:T(8,128)(2,1)} %fusion), kind=kOutput, calls=%fused_computation.13 | convolution fusion | flops 9617801216 | bytes 35586048 | tf_op jit(solution)/shard_map/td,fd->tf/dot_general | solution.py:69
  175.0 0.0 copy-start.4
  175.0 2.2 copy-done.4
  177.3 15.2 %convolution_convert_fusion = bf16[4864,1920]{1,0:T(8,128)(2,1)} fusion(bf16[512,4864]{1,0:T(8,128)(2,1)S(1)} %get-tuple-element.5, bf16[512,1920]{1,0:T(8,128)(2,1)S(1)} %copy-done.1), kind=kOutput, calls=%fused_computation.2 | convolution fusion | flops 9572352000 | bytes 25624576 | tf_op jit(solution)/shard_map/dot_general | solution.py:74
  192.5 0.0 reduce-scatter.2.cloned.1.call-update
  192.5 0.0 all-reduce.2.cloned.1.call-start
  192.6 203.4 %reduce-scatter.2.cloned.1.call-done = bf16[304,1920]{1,0:T(8,128)(2,1)} async-done(((bf16[4864,1920]{1,0:T(8,128)(2,1)}), bf16[304,1920]{1,0:T(8,128)(2,1)}) %reduce-scatter.2.cloned.1.call-update) | async-done | bytes 1167376 | tf_op jit(solution)/shard_map/reduce_scatter | solution.py:78
  396.0 0.0 all-reduce.2.cloned.1.call-update
  396.0 17.9 %multiply_reduce_fusion.2 = (f32[2,256]{1,0:T(2,128)S(1)}, f32[2,256]{1,0:T(2,128)S(1)}, f32[2,256,1920]{2,1,0:T(8,128)}) fusion(f32[2,1920]{1,0:T(2,128)S(1)} %get-tuple-element.7, f32[2,256]{1,0:T(2,128)S(1)} %rsqrt.13, f32[2,256]{1,0:T(2,128)S(1)} %div.17, bf16[2,256,4864]{2,1,0:T(8,128)(2,1)} %bitcast.52, bf16[4864,1920]{0,1:T(8,128)(2,1)} %fusion, ...), kind=kOutput, calls=%fused_computation.22 | convolution fusion | flops 9569894400 | bytes 29580288 | tf_op jit(solution)/shard_map/dot_general | solution.py:73
  413.9 3.9 multiply_convert_fusion.1
  417.7 69.2 %all-reduce.2.cloned.1.call-done = bf16[304,1920]{1,0:T(8,128)(2,1)} async-done(((bf16[304,1920]{1,0:T(8,128)(2,1)}), bf16[304,1920]{1,0:T(8,128)(2,1)}) %all-reduce.2.cloned.1.call-update) | async-done | bytes 1167376 | tf_op jit(solution)/shard_map/psum | solution.py:81
  487.0 2.8 convert_element_type.48
  (7 shorter events, 0.1 us)
Async XLA Ops:
  7.2 23.7 %copy-start = (bf16[512,1920]{1,0:T(8,128)(2,1)S(1)}, bf16[512,1920]{1,0:T(8,128)(2,1)}, u32[]{:S(2)}) copy-start(bf16[512,1920]{1,0:T(8,128)(2,1)} %param.6) | copy-start | bytes 5898244
  7.2 24.8 %copy-start.3 = (s32[2]{0:T(128)S(1)}, s32[2]{0:T(128)}, u32[]{:S(2)}) copy-start(s32[2]{0:T(128)} %param.7) | copy-start | bytes 28
  7.2 105.7 %all-gather.3.cloned.1.call-start = ((), (), s32[]{:S(2)}) async-start(), calls=%async_computation.1 | async-start | bytes 19845120 | tf_op jit(solution)/shard_map/all_gather | solution.py:65
  7.9 388.0 %reduce-scatter.2.cloned.1.call-start = ((), (), s32[]{:S(2)}) async-start(), calls=%async_computation.2 | async-start | bytes 19845120 | tf_op jit(solution)/shard_map/reduce_scatter | solution.py:78
  30.9 1.2 copy-start.2
  136.2 17.3 %copy-start.1 = (bf16[512,1920]{1,0:T(8,128)(2,1)S(1)}, bf16[512,1920]{1,0:T(8,128)(2,1)}, u32[]{:S(2)}) copy-start(bf16[512,1920]{1,0:T(8,128)(2,1)} %fusion.10) | copy-start | bytes 5898244
  175.0 2.2 copy-start.4
  192.5 294.4 %all-reduce.2.cloned.1.call-start = ((), (), s32[]{:S(2)}) async-start(), calls=%async_computation.3 | async-start | bytes 2334720 | tf_op jit(solution)/shard_map/psum | solution.py:81
Sparse Core Ops, SparseCore 0:
  9.7 103.0 all-gather.2
  192.6 203.2 reduce-scatter.1
  398.6 88.2 all-reduce.1
where the time goes:
time: 497 us; the launch traced here: 496 us
  waiting for transfers between devices  351 us (71%)
  matrix products  55.1 us (11%)
  other arithmetic  27.5 us (6%)
  local copies, waits for them, and re-layouts  26 us (5%)
  blocking collectives  22.6 us (5%)
  between operations  13.8 us (3%)
    reduce_scatter x1, waiting for transfers between devices, per_device(): lax.psum_scatter(rounded.astype(jnp.float32).astype(jnp.bfloat16), 'shard...  203 us
    all_gather x1, waiting for transfers between devices, per_device(): lax.all_gather(weight_values, 'shard', axis=0, tiled=True)  77.8 us
    psum x1, waiting for transfers between devices, per_device(): grad_weight = lax.psum(group_part, 'replica').astype(jnp.float32)  69.2 us
    all_gather x1, local copies, waits for them, and re-layouts, per_device(): lax.all_gather(weight_values, 'shard', axis=0, tiled=True)  23.3 us
    all_gather x1, blocking collectives, per_device(): lax.all_gather(weight_scales, 'shard', axis=0, tiled=True)  22.6 us
    dot_general x1, matrix products, per_device(): jnp.einsum('td,fd->tf', moved, weight, preferred_element_type=jnp.float32)  21.5 us
    dot_general x1, matrix products, per_device(): grad_moved = jnp.dot(grad_pre, weight, preferred_element_type=jnp.float32)  17.9 us
    convert_element_type x1, other arithmetic, dequantize(): return expanded.reshape(row_count, features).astype(jnp.bfloat16)  17.3 us
  transfers between devices with their start and end apart: 3, of which 3 were waited for; matrix products, arithmetic and copies ran while one was open for 5% of the time, Pallas kernels for 0%

commit v1 on v0

--- a/solution.py
+++ b/solution.py
@@ -61,11 +61,9 @@
 def per_device(tokens, timesteps, table, weight_values, weight_scales, cotangent):
     moved, normed, inverse, factor = modulate(tokens, timesteps, table)
     upstream = cotangent.astype(jnp.float32)
-    gathered_values, gathered_scales = (
-        lax.all_gather(weight_values, "shard", axis=0, tiled=True),
-        lax.all_gather(weight_scales, "shard", axis=0, tiled=True),
+    weight = lax.all_gather(
+        dequantize(weight_values, weight_scales), "shard", axis=0, tiled=True
     )
-    weight = dequantize(gathered_values, gathered_scales)
     preact = jnp.einsum("td,fd->tf", moved, weight, preferred_element_type=jnp.float32)
     gelu_value, derivative = gelu_slope(preact)
     hidden = gelu_value.astype(jnp.bfloat16)

time: 497 us -> 462 us (0.930)
  local copies, waits for them, and re-layouts: 26 us -> 1.69 us
  blocking collectives: 22.6 us -> 0 us
  waiting for transfers between devices: 351 us -> 368 us
  other arithmetic: 27.5 us -> 11.8 us
  matrix products: 55.1 us -> 66.3 us
    all_gather x1 -> x0, local copies, waits for them, and re-layouts: 23.3 us -> none  [per_device(): lax.all_gather(weight_values, 'shard', axis=0, tiled=True)]
    all_gather x1 -> x0, blocking collectives: 22.6 us -> none  [per_device(): lax.all_gather(weight_scales, 'shard', axis=0, tiled=True)]
    all_gather x1, waiting for transfers between devices: 77.8 us -> 99.2 us  [per_device(): lax.all_gather(dequantize(weight_values, weight_scales), 'shard', axis=0,...]
    convert_element_type x1, other arithmetic: 17.3 us -> 3.1 us  [dequantize(): return expanded.reshape(row_count, features).astype(jnp.bfloat16)]
    dot_general x1, matrix products: 15.2 us -> 23.2 us  [per_device(): lax.dot_general(grad_pre, moved, (((0,), (0,)), ((), ())), preferred_elem...]
    dot_general x1, matrix products: 17.9 us -> 23.9 us  [per_device(): grad_moved = jnp.dot(grad_pre, weight, preferred_element_type=jnp.float32)]
  transfers between devices with their start and end apart: 3 -> 3, of which waited for: 3 -> 3; matrix products, arithmetic and copies ran while one was open for 5% -> 7% of each run, Pallas kernels for 0% -> 0%
where the time goes in v1:
time: 462 us; the launch traced here: 461 us
  waiting for transfers between devices  368 us (80%)
  matrix products  66.3 us (14%)
  between operations  13.8 us (3%)
  other arithmetic  11.8 us (3%)
    reduce_scatter x1, waiting for transfers between devices, per_device(): lax.psum_scatter(rounded.astype(jnp.float32).astype(jnp.bfloat16), 'shard...  203 us
    all_gather x1, waiting for transfers between devices, per_device(): lax.all_gather(dequantize(weight_values, weight_scales), 'shard', axis=0,...  99.2 us
    psum x1, waiting for transfers between devices, per_device(): grad_weight = lax.psum(group_part, 'replica').astype(jnp.float32)  65.1 us
    dot_general x1, matrix products, per_device(): grad_moved = jnp.dot(grad_pre, weight, preferred_element_type=jnp.float32)  23.9 us
    dot_general x1, matrix products, per_device(): lax.dot_general(grad_pre, moved, (((0,), (0,)), ((), ())), preferred_elem...  23.2 us
    dot_general x1, matrix products, per_device(): jnp.einsum('td,fd->tf', moved, weight, preferred_element_type=jnp.float32)  18.7 us
  transfers between devices with their start and end apart: 3, of which 3 were waited for; matrix products, arithmetic and copies ran while one was open for 7% of the time, Pallas kernels for 0%

profile of v1, /device:TPU:0, one launch (start us, length us, event | category | flops | bytes accessed | tf_op | source)
XLA Modules:
  0.0 461.4 jit_solution(8686879250005387591)
XLA Ops:
  7.2 0.0 copy-start
  7.2 0.0 copy-start.1
  7.2 0.0 copy-start.2
  7.2 0.0 all-gather.2.cloned.1.call-start
  7.2 1.0 copy.11
  8.2 0.7 mul.124
  8.9 3.1 fusion.18
  12.0 0.0 all-gather.2.cloned.1.call-update
  12.0 0.0 reduce-scatter.2.cloned.1.call-start
  12.1 0.0 copy-done
  12.1 0.3 convert_reduce_fusion
  12.4 0.7 fusion.15
  13.1 0.0 copy-done.1
  13.1 0.0 copy-done.2
  13.1 0.4 fusion.19
  13.6 2.5 fusion.17
  16.1 99.2 %all-gather.2.cloned.1.call-done = bf16[4864,1920]{1,0:T(8,128)(2,1)} async-done(((bf16[304,1920]{1,0:T(8,128)(2,1)}), bf16[4864,1920]{1,0:T(8,128)(2,1)}) %all-gather.2.cloned.1.call-update) | async-done | bytes 18677776 | tf_op jit(solution)/shard_map/all_gather | solution.py:64
  115.3 18.7 %multiply_convert_fusion = (bf16[512,4864]{1,0:T(8,128)(2,1)}, f32[512,4864]{1,0:T(8,128)}) fusion(bf16[512,1920]{1,0:T(8,128)(2,1)} %fusion.17, bf16[4864,1920]{1,0:T(8,128)(2,1)} %all-gather.2.cloned.1.call-done), kind=kOutput, calls=%fused_computation.10 | convolution fusion | flops 9585426432 | bytes 35586048 | tf_op jit(solution)/shard_map/td,fd->tf/dot_general | solution.py:67
  134.0 23.2 %convolution_convert_fusion = bf16[4864,1920]{1,0:T(8,128)(2,1)} fusion(bf16[512,1920]{1,0:T(8,128)(2,1)} %fusion.17, f32[512,4864]{1,0:T(8,128)} %get-tuple-element.8, bf16[512,4864]{1,0:T(8,128)(2,1)} %param.11), kind=kOutput, calls=%fused_computation | convolution fusion | flops 9622159360 | bytes 35586048 | tf_op jit(solution)/shard_map/dot_general | solution.py:72
  157.2 0.0 reduce-scatter.2.cloned.1.call-update
  157.2 0.0 all-reduce.2.cloned.1.call-start
  157.3 203.4 %reduce-scatter.2.cloned.1.call-done = bf16[304,1920]{1,0:T(8,128)(2,1)} async-done(((bf16[4864,1920]{1,0:T(8,128)(2,1)}), bf16[304,1920]{1,0:T(8,128)(2,1)}) %reduce-scatter.2.cloned.1.call-update) | async-done | bytes 1167376 | tf_op jit(solution)/shard_map/reduce_scatter | solution.py:76
  360.7 0.0 all-reduce.2.cloned.1.call-update
  360.7 23.9 %fusion.29 = (f32[512]{0:T(512)S(1)}, f32[512]{0:T(512)S(1)}, f32[512,1920]{1,0:T(8,128)S(1)}) fusion(f32[512]{0:T(512)S(1)} %add_rsqrt_fusion, f32[512]{0:T(512)S(1)} %broadcast_multiply_fusion.2, bf16[512,1920]{1,0:T(8,128)(2,1)S(1)} %copy-done, f32[2,1920]{1,0:T(2,128)S(1)} %get-tuple-element.5, bf16[4864,1920]{1,0:T(8,128)(2,1)} %all-gather.2.cloned.1.call-done, ...), kind=kOutput, calls=%fused_computation.42 | convolution fusion | flops 9619701760 | bytes 39541760 | tf_op jit(solution)/shard_map/dot_general | solution.py:71
  384.6 2.4 fusion.14
  387.0 65.1 %all-reduce.2.cloned.1.call-done = bf16[304,1920]{1,0:T(8,128)(2,1)} async-done(((bf16[304,1920]{1,0:T(8,128)(2,1)}), bf16[304,1920]{1,0:T(8,128)(2,1)}) %all-reduce.2.cloned.1.call-update) | async-done | bytes 1167376 | tf_op jit(solution)/shard_map/psum | solution.py:79
  452.1 2.8 convert_element_type.45
  (4 shorter events, 0.0 us)
Async XLA Ops:
  7.2 4.9 %copy-start = (bf16[512,1920]{1,0:T(8,128)(2,1)S(1)}, bf16[512,1920]{1,0:T(8,128)(2,1)}, u32[]{:S(2)}) copy-start(bf16[512,1920]{1,0:T(8,128)(2,1)} %param.6) | copy-start | bytes 5898244
  7.2 5.9 %copy-start.1 = (f32[64,2,1920]{2,1,0:T(2,128)S(1)}, f32[64,2,1920]{2,1,0:T(2,128)}, u32[]{:S(2)}) copy-start(f32[64,2,1920]{2,1,0:T(2,128)} %param.8) | copy-start | bytes 2949124
  7.2 5.9 %copy-start.2 = (s32[2]{0:T(128)S(1)}, s32[2]{0:T(128)}, u32[]{:S(2)}) copy-start(s32[2]{0:T(128)} %param.7) | copy-start | bytes 28
  7.2 108.1 %all-gather.2.cloned.1.call-start = ((), (), s32[]{:S(2)}) async-start(), calls=%async_computation.1 | async-start | bytes 19845120 | tf_op jit(solution)/shard_map/all_gather | solution.py:64
  12.0 348.6 %reduce-scatter.2.cloned.1.call-start = ((), (), s32[]{:S(2)}) async-start(), calls=%async_computation.2 | async-start | bytes 19845120 | tf_op jit(solution)/shard_map/reduce_scatter | solution.py:76
  157.2 294.8 %all-reduce.2.cloned.1.call-start = ((), (), s32[]{:S(2)}) async-start(), calls=%async_computation.3 | async-start | bytes 2334720 | tf_op jit(solution)/shard_map/psum | solution.py:79
Sparse Core Ops, SparseCore 0:
  12.2 103.0 all-gather.1
  157.4 203.2 reduce-scatter.1
  363.4 88.6 all-reduce.1

commit v2 on v1

--- a/solution.py
+++ b/solution.py
@@ -1,6 +1,8 @@
 import jax
 import jax.numpy as jnp
 from jax import lax
+from jax.experimental import pallas as pl
+from jax.experimental.pallas import tpu as pltpu
 from jax.sharding import PartitionSpec as P
 
 root_two_over_pi = 0.7978845608028654
@@ -58,6 +60,300 @@
     return result.reshape(-1, features).astype(jnp.bfloat16)
 
 
+MESH = pl.DeviceIdType.MESH
+KS = (1, 3, 2)
+Z_ROWS, X_ROWS, Y_ROWS = 112, 96, 96
+X_AT, Y_AT = Z_ROWS, Z_ROWS + X_ROWS
+OWN_ROWS = Z_ROWS + X_ROWS + Y_ROWS
+
+
+def flip(value, k):
+    low, high = value % 2, value // 2
+    if k & 1:
+        low = 1 - low
+    if k & 2:
+        high = 1 - high
+    return 2 * high + low
+
+
+def place():
+    replica, shard = lax.axis_index("replica"), lax.axis_index("shard")
+    return (replica // 2, 2 * (replica % 2) + (shard // 2) % 2, shard // 4, shard % 2)
+
+
+def device_at(x, y, z, core):
+    return (2 * x + y // 2, (2 * z + y % 2) * 2 + core)
+
+
+def quarter(x):
+    return pl.multiple_of(jnp.minimum(512 * x, 1408), 128)
+
+
+def half(y):
+    return pl.multiple_of(896 * (y // 2), 128)
+
+
+def part(v):
+    return pl.multiple_of(256 * v, 128)
+
+
+def add_rows(rows, store, loads):
+    def body(step, _):
+        at = pl.ds(pl.multiple_of(step * 16, 16), 16)
+        total = loads[0](at).astype(jnp.float32)
+        for load in loads[1:]:
+            total = total + load(at).astype(jnp.float32)
+        store(at, total)
+        return 0
+
+    lax.fori_loop(0, rows // 16, body, 0)
+
+
+def reduce_kernel(
+    product, out, own, other, zr1, zr2, zr3, xr1, xr2, xr3, yr1, yr2, yr3,
+    zb, zc, xb, xc, yb, yc, pieces, local_sem, core_sem, s1, r1, s2, r2, s3, r3, s4, r4,
+):
+    x, y, z, core = place()
+
+    def to(dx=0, dy=0, dz=0, dc=0):
+        return device_at(flip(x, dx), flip(y, dy), flip(z, dz), 1 - core if dc else core)
+
+    peers = [to(dc=1)]
+    peers += [to(dx=k) for k in KS] + [to(dy=k) for k in KS] + [to(dz=k) for k in KS]
+    peers += [to(dx=k, dy=2) for k in KS]
+    barrier = pltpu.get_barrier_semaphore()
+    for peer in peers:
+        pl.semaphore_signal(barrier, inc=1, device_id=peer, device_id_type=MESH)
+    pl.semaphore_wait(barrier, len(peers))
+
+    started = []
+
+    def send(src, dst, send_sem, recv_sem, peer):
+        copy = pltpu.make_async_remote_copy(
+            src_ref=src, dst_ref=dst, send_sem=send_sem, recv_sem=recv_sem,
+            device_id=peer, device_id_type=MESH,
+        )
+        copy.start()
+        started.append(copy)
+        return copy
+
+    order = [(zi, yi) for zi in (1, 3, 2, 0) for yi in (1, 0)]
+    swaps = {}
+    for n, (zi, yi) in enumerate(order):
+        block = 2 * flip(z, zi) + flip(y, yi) % 2
+        mine = pltpu.make_async_copy(
+            product.at[2 * block + core], own.at[zi, yi], local_sem.at[n]
+        )
+        mine.start()
+        theirs = send(
+            product.at[2 * block + 1 - core], other.at[zi, yi],
+            core_sem.at[0, n], core_sem.at[1, n], to(dc=1),
+        )
+        swaps[zi, yi] = (mine, theirs)
+
+    first = {"z": [], "x": [], "y": []}
+    for zi, yi in order:
+        mine, theirs = swaps[zi, yi]
+        mine.wait()
+        theirs.wait_recv()
+        mine_ref, other_ref = own.at[zi, yi], other.at[zi, yi]
+
+        def keep(at, total, mine_ref=mine_ref):
+            mine_ref[at, :] = total.astype(jnp.bfloat16)
+
+        add_rows(
+            OWN_ROWS, keep,
+            [lambda at, ref=mine_ref: ref[at, :], lambda at, ref=other_ref: ref[at, :]],
+        )
+        if zi:
+            n = (zi - 1) * 2 + yi
+            first["z"].append(send(
+                own.at[zi, yi, pl.ds(0, Z_ROWS), :], zr1.at[zi - 1, yi],
+                s1.at[n], r1.at[n], to(dz=zi),
+            ))
+        for k in KS:
+            n = 6 + (zi * 2 + yi) * 3 + k - 1
+            first["x"].append(send(
+                own.at[zi, yi, pl.ds(X_AT, X_ROWS), pl.ds(quarter(flip(x, k)), 512)],
+                xr1.at[k - 1, zi, yi], s1.at[n], r1.at[n], to(dx=k),
+            ))
+        for k in (1, 3) if yi else (2,):
+            n = 30 + zi * 3 + k - 1
+            first["y"].append(send(
+                own.at[zi, yi, pl.ds(Y_AT, Y_ROWS), pl.ds(half(flip(y, k)), 1024)],
+                yr1.at[k - 1, zi], s1.at[n], r1.at[n], to(dy=k),
+            ))
+
+    def store_to(ref):
+        def store(at, total):
+            ref[at, :] = total.astype(jnp.bfloat16)
+
+        return store
+
+    def shifted(ref, base, columns):
+        return lambda at: ref[pl.ds(base + at.start, at.size), columns]
+
+    def plain(ref):
+        return lambda at: ref[at, :]
+
+    second = {"z": [], "x": [], "y": []}
+    for copy in first["z"]:
+        copy.wait_recv()
+    for yi in (0, 1):
+        add_rows(
+            Z_ROWS, store_to(zb.at[yi]),
+            [plain(own.at[0, yi])] + [plain(zr1.at[k - 1, yi]) for k in KS],
+        )
+    for k in KS:
+        second["z"].append(send(
+            zb.at[:, :, pl.ds(quarter(flip(x, k)), 512)], zr2.at[k - 1],
+            s2.at[k - 1], r2.at[k - 1], to(dx=k),
+        ))
+    for copy in first["y"]:
+        copy.wait_recv()
+    for zi in (1, 3, 2, 0):
+        columns = pl.ds(half(y), 1024)
+        add_rows(
+            Y_ROWS, store_to(yb.at[zi]),
+            [shifted(own.at[zi, 0], Y_AT, columns)] + [plain(yr1.at[k - 1, zi]) for k in KS],
+        )
+        if zi:
+            second["y"].append(send(
+                yb.at[zi], yr2.at[zi - 1], s2.at[2 + zi], r2.at[2 + zi], to(dz=zi)
+            ))
+    for copy in first["x"]:
+        copy.wait_recv()
+    for yi in (1, 0):
+        for zi in range(4):
+            columns = pl.ds(quarter(x), 512)
+            add_rows(
+                X_ROWS, store_to(xb.at[zi, yi]),
+                [shifted(own.at[zi, yi], X_AT, columns)]
+                + [plain(xr1.at[k - 1, zi, yi]) for k in KS],
+            )
+        for k in (1, 3) if yi else (2,):
+            second["x"].append(send(
+                xb.at[:, yi, :, pl.ds(part(flip(y, k) // 2), 256)], xr2.at[k - 1],
+                s2.at[5 + k], r2.at[5 + k], to(dy=k),
+            ))
+
+    third = {"z": [], "x": [], "y": []}
+    for copy in second["z"]:
+        copy.wait_recv()
+    for yi in (1, 0):
+        columns = pl.ds(quarter(x), 512)
+        add_rows(
+            Z_ROWS, store_to(zc.at[yi]),
+            [shifted(zb.at[yi], 0, columns)] + [plain(zr2.at[k - 1, yi]) for k in KS],
+        )
+        for k in (1, 3) if yi else (2,):
+            third["z"].append(send(
+                zc.at[yi, :, pl.ds(part(flip(y, k) // 2), 256)], zr3.at[k - 1],
+                s3.at[k - 1], r3.at[k - 1], to(dy=k),
+            ))
+    for copy in second["y"]:
+        copy.wait_recv()
+    add_rows(Y_ROWS, store_to(yc), [plain(yb.at[0])] + [plain(yr2.at[k - 1]) for k in KS])
+    for k in KS:
+        third["y"].append(send(
+            yc.at[:, pl.ds(part(flip(x, k)), 256)], yr3.at[k - 1],
+            s3.at[2 + k], r3.at[2 + k], to(dx=k),
+        ))
+    for copy in second["x"]:
+        copy.wait_recv()
+    for zi in (1, 3, 2, 0):
+        columns = pl.ds(part(y // 2), 256)
+        add_rows(
+            X_ROWS, store_to(xc.at[zi]),
+            [shifted(xb.at[zi, 0], 0, columns)] + [plain(xr2.at[k - 1, zi]) for k in KS],
+        )
+        if zi:
+            third["x"].append(send(
+                xc.at[zi], xr3.at[zi - 1], s3.at[5 + zi], r3.at[5 + zi], to(dz=zi)
+            ))
+
+    def store_piece(base):
+        def store(at, total):
+            pieces[0, pl.ds(base + at.start, at.size), :] = total.astype(jnp.bfloat16)
+
+        return store
+
+    for copy in third["z"]:
+        copy.wait_recv()
+    columns = pl.ds(part(y // 2), 256)
+    add_rows(
+        Z_ROWS, store_piece(0),
+        [shifted(zc.at[0], 0, columns)] + [plain(zr3.at[k - 1]) for k in KS],
+    )
+    for copy in third["y"]:
+        copy.wait_recv()
+    own_columns = pl.ds(part(x), 256)
+    add_rows(
+        Y_ROWS, store_piece(Y_AT),
+        [shifted(yc, 0, own_columns)] + [plain(yr3.at[k - 1]) for k in KS],
+    )
+    for copy in third["x"]:
+        copy.wait_recv()
+    add_rows(
+        X_ROWS, store_piece(X_AT), [plain(xc.at[0])] + [plain(xr3.at[k - 1]) for k in KS]
+    )
+
+    spread = []
+    for dx in (0, 1, 3, 2):
+        for dy in (2, 0):
+            if dx or dy:
+                n = 2 * dx + dy // 2
+                spread.append(send(
+                    pieces.at[0], pieces.at[n], s4.at[n - 1], r4.at[n - 1], to(dx=dx, dy=dy)
+                ))
+    for copy in spread:
+        copy.wait_recv()
+    for px in range(4):
+        for ph in range(2):
+            lows = (px % 2 + x % 2) % 2
+            highs = (px // 2 + x // 2) % 2
+            slot = 2 * (2 * highs + lows) + (ph + y // 2) % 2
+            at = min(512 * px, 1408) + 256 * ph
+            out[0:Y_AT, at : at + 256] = pieces[slot, 0:Y_AT, :].astype(jnp.float32)
+    for ph in range(2):
+        for px in range(4):
+            lows = (px % 2 + x % 2) % 2
+            highs = (px // 2 + x // 2) % 2
+            slot = 2 * (2 * highs + lows) + (ph + y // 2) % 2
+            at = 896 * ph + 256 * px
+            out[Y_AT:OWN_ROWS, at : at + 256] = pieces[slot, Y_AT:OWN_ROWS, :].astype(jnp.float32)
+    for copy in started:
+        copy.wait_send()
+
+
+def reduce_blocks(product):
+    features = product.shape[1]
+    bf16 = jnp.bfloat16
+    shapes = [
+        (4, 2, OWN_ROWS, features), (4, 2, OWN_ROWS, features),
+        (3, 2, Z_ROWS, features), (3, 2, Z_ROWS, 512), (3, Z_ROWS, 256),
+        (3, 4, 2, X_ROWS, 512), (3, 4, X_ROWS, 256), (3, X_ROWS, 256),
+        (3, 4, Y_ROWS, 1024), (3, Y_ROWS, 1024), (3, Y_ROWS, 256),
+        (2, Z_ROWS, features), (2, Z_ROWS, 512),
+        (4, 2, X_ROWS, 512), (4, X_ROWS, 256),
+        (4, Y_ROWS, 1024), (Y_ROWS, 1024),
+        (8, OWN_ROWS, 256),
+    ]
+    sems = [(8,), (2, 8), (42,), (42,), (9,), (9,), (9,), (9,), (7,), (7,)]
+    return pl.pallas_call(
+        reduce_kernel,
+        out_shape=jax.ShapeDtypeStruct((OWN_ROWS, features), jnp.float32),
+        in_specs=[pl.BlockSpec(memory_space=pl.ANY)],
+        out_specs=pl.BlockSpec(memory_space=pltpu.VMEM),
+        scratch_shapes=[pltpu.VMEM(shape, bf16) for shape in shapes]
+        + [pltpu.SemaphoreType.DMA(shape) for shape in sems],
+        compiler_params=pltpu.CompilerParams(
+            collective_id=0, has_side_effects=True, vmem_limit_bytes=56 << 20
+        ),
+        name="reduce_blocks",
+    )(product.reshape(-1, OWN_ROWS, features))
+
+
 def per_device(tokens, timesteps, table, weight_values, weight_scales, cotangent):
     moved, normed, inverse, factor = modulate(tokens, timesteps, table)
     upstream = cotangent.astype(jnp.float32)
@@ -72,11 +368,7 @@
     product = lax.dot_general(
         grad_pre, moved, (((0,), (0,)), ((), ())), preferred_element_type=jnp.float32
     )
-    rounded = lax.optimization_barrier(product.astype(jnp.bfloat16))
-    group_part = lax.psum_scatter(
-        rounded.astype(jnp.float32).astype(jnp.bfloat16), "shard", scatter_dimension=0, tiled=True
-    )
-    grad_weight = lax.psum(group_part, "replica").astype(jnp.float32)
+    grad_weight = reduce_blocks(product.astype(jnp.bfloat16))
     grad_tokens = normalize_back(grad_moved, normed, inverse, factor)
     return (hidden, grad_weight, grad_tokens)
 

time: 462 us -> 280 us (0.61)
  waiting for transfers between devices: 368 us -> 99.3 us
  Pallas kernels: 0 us -> 88.5 us
    reduce_scatter x1 -> x0, waiting for transfers between devices: 203 us -> none  [per_device(): lax.psum_scatter(rounded.astype(jnp.float32).astype(jnp.bfloat16), 'shard...]
    pallas_call x0 -> x1, Pallas kernels: none -> 88.5 us  [reduce_blocks(): pl.pallas_call(reduce_kernel, out_shape=jax.ShapeDtypeStruct((OWN_ROWS, f...]
    psum x1 -> x0, waiting for transfers between devices: 65.1 us -> none  [per_device(): grad_weight = lax.psum(group_part, 'replica').astype(jnp.float32)]
  transfers between devices with their start and end apart: 3 -> 1, of which waited for: 3 -> 1; matrix products, arithmetic and copies ran while one was open for 7% -> 1% of each run, Pallas kernels for 0% -> 0%
where the time goes in v2:
time: 280 us
  waiting for transfers between devices  99.3 us (35%)
  Pallas kernels  88.5 us (32%)
  matrix products  66.1 us (24%)
  between operations  14.1 us (5%)
  other arithmetic  8.95 us (3%)
  local copies, waits for them, and re-layouts  3.09 us (1%)
    all_gather x1, waiting for transfers between devices, per_device(): lax.all_gather(dequantize(weight_values, weight_scales), 'shard', axis=0,...  99.3 us
    pallas_call x1, Pallas kernels, reduce_blocks(): pl.pallas_call(reduce_kernel, out_shape=jax.ShapeDtypeStruct((OWN_ROWS, f...  88.5 us
    dot_general x1, matrix products, per_device(): grad_moved = jnp.dot(grad_pre, weight, preferred_element_type=jnp.float32)  23.8 us
    dot_general x1, matrix products, per_device(): lax.dot_general(grad_pre, moved, (((0,), (0,)), ((), ())), preferred_elem...  23.2 us
    dot_general x1, matrix products, per_device(): jnp.einsum('td,fd->tf', moved, weight, preferred_element_type=jnp.float32)  18.7 us
  transfers between devices with their start and end apart: 1, of which 1 were waited for; matrix products, arithmetic and copies ran while one was open for 1% of the time, Pallas kernels for 0%

profile of v2, /device:TPU:0, one launch (start us, length us, event | category | flops | bytes accessed | tf_op | source)
XLA Modules:
  0.0 280.1 jit_solution(8581757598786269427)
XLA Ops:
  7.2 0.0 copy-start
  7.2 0.0 copy-start.2
  7.2 0.0 copy-start.3
  7.2 0.0 all-gather.2.cloned.1.call-start
  7.2 1.0 copy.11
  8.2 0.7 mul.124
  8.9 3.1 %fusion.18 = bf16[304,1920]{1,0:T(8,128)(2,1)} fusion(f32[38,8,15,128]{3,2,1,0:T(8,128)S(1)} %bitcast.38, bf16[304,1920]{1,0:T(8,128)(2,1)} %param.9), kind=kLoop, calls=%fused_computation.27 | loop fusion | flops 1751040 | bytes 4669440 | tf_op jit(solution)/shard_map/convert_element_type | solution.py:30
  12.0 0.0 all-gather.2.cloned.1.call-update
  12.0 0.0 copy-done
  12.1 0.3 convert_reduce_fusion
  12.4 0.7 fusion.15
  13.1 0.0 copy-done.2
  13.1 0.0 copy-done.3
  13.1 0.4 fusion.19
  13.5 2.5 fusion.17
  16.0 99.3 %all-gather.2.cloned.1.call-done = bf16[4864,1920]{1,0:T(8,128)(2,1)} async-done(((bf16[304,1920]{1,0:T(8,128)(2,1)}), bf16[4864,1920]{1,0:T(8,128)(2,1)}) %all-gather.2.cloned.1.call-update) | async-done | bytes 18677776 | tf_op jit(solution)/shard_map/all_gather | solution.py:360
  115.3 18.7 %multiply_convert_fusion = (bf16[512,4864]{1,0:T(8,128)(2,1)}, f32[512,4864]{1,0:T(8,128)}) fusion(bf16[512,1920]{1,0:T(8,128)(2,1)} %fusion.17, bf16[4864,1920]{1,0:T(8,128)(2,1)} %all-gather.2.cloned.1.call-done), kind=kOutput, calls=%fused_computation.10 | convolution fusion | flops 9585426432 | bytes 35586048 | tf_op jit(solution)/shard_map/td,fd->tf/dot_general | solution.py:363
  134.0 23.2 %convolution_convert_fusion = bf16[4864,1920]{1,0:T(8,128)(2,1)} fusion(bf16[512,1920]{1,0:T(8,128)(2,1)} %fusion.17, f32[512,4864]{1,0:T(8,128)} %get-tuple-element.8, bf16[512,4864]{1,0:T(8,128)(2,1)} %param.11), kind=kOutput, calls=%fused_computation | convolution fusion | flops 9622159360 | bytes 35586048 | tf_op jit(solution)/shard_map/dot_general | solution.py:368
  157.2 88.5 %reduce_blocks.1 = f32[304,1920]{1,0:T(8,128)} custom-call(bf16[16,304,1920]{2,1,0:T(8,128)(2,1)} %bitcast.37), custom_call_target="tpu_custom_call" | custom-call | tf_op jit(solution)/shard_map/reduce_blocks/pallas_call | solution.py:343
  245.7 0.0 copy-start.1
  245.7 23.8 %fusion.29 = (f32[512]{0:T(512)S(1)}, f32[512]{0:T(512)S(1)}, f32[512,1920]{1,0:T(8,128)S(1)}) fusion(f32[512]{0:T(512)S(1)} %add_rsqrt_fusion, f32[512]{0:T(512)S(1)} %broadcast_multiply_fusion.2, bf16[512,1920]{1,0:T(8,128)(2,1)S(1)} %copy-done, f32[2,1920]{1,0:T(2,128)S(1)} %get-tuple-element.5, bf16[4864,1920]{1,0:T(8,128)(2,1)} %all-gather.2.cloned.1.call-done, ...), kind=kOutput, calls=%fused_computation.42 | convolution fusion | flops 9619701760 | bytes 39541760 | tf_op jit(solution)/shard_map/dot_general | solution.py:367
  269.5 2.4 fusion.14
  271.9 0.0 copy-done.1
  271.9 1.4 copy.24
  (4 shorter events, 0.0 us)
Async XLA Ops:
  7.2 4.9 %copy-start = (bf16[512,1920]{1,0:T(8,128)(2,1)S(1)}, bf16[512,1920]{1,0:T(8,128)(2,1)}, u32[]{:S(2)}) copy-start(bf16[512,1920]{1,0:T(8,128)(2,1)} %param.6) | copy-start | bytes 5898244
  7.2 5.9 %copy-start.2 = (f32[64,2,1920]{2,1,0:T(2,128)S(1)}, f32[64,2,1920]{2,1,0:T(2,128)}, u32[]{:S(2)}) copy-start(f32[64,2,1920]{2,1,0:T(2,128)} %param.8) | copy-start | bytes 2949124
  7.2 5.9 %copy-start.3 = (s32[2]{0:T(128)S(1)}, s32[2]{0:T(128)}, u32[]{:S(2)}) copy-start(s32[2]{0:T(128)} %param.7) | copy-start | bytes 28
  7.2 108.1 %all-gather.2.cloned.1.call-start = ((), (), s32[]{:S(2)}) async-start(), calls=%async_computation | async-start | bytes 19845120 | tf_op jit(solution)/shard_map/all_gather | solution.py:360
  245.7 26.2 %copy-start.1 = (f32[304,1920]{1,0:T(8,128)S(1)}, f32[304,1920]{1,0:T(8,128)}, u32[]{:S(2)}) copy-start(f32[304,1920]{1,0:T(8,128)} %reduce_blocks.1) | copy-start | bytes 7004164
Sparse Core Ops, SparseCore 0:
  12.2 103.0 all-gather.1

commit v3 on v2

--- a/solution.py
+++ b/solution.py
@@ -65,6 +65,7 @@
 Z_ROWS, X_ROWS, Y_ROWS = 112, 96, 96
 X_AT, Y_AT = Z_ROWS, Z_ROWS + X_ROWS
 OWN_ROWS = Z_ROWS + X_ROWS + Y_ROWS
+WINDOWS = ((0, 1024), (1024, 1024), (2048, 1024), (3072, 1024), (4096, 768))
 
 
 def flip(value, k):
@@ -110,8 +111,9 @@
 
 
 def reduce_kernel(
-    product, out, own, other, zr1, zr2, zr3, xr1, xr2, xr3, yr1, yr2, yr3,
-    zb, zc, xb, xc, yb, yc, pieces, local_sem, core_sem, s1, r1, s2, r2, s3, r3, s4, r4,
+    gradient_rows, gradient, moved, weight, out, grad_moved, own, operand, tokens_all,
+    weight_parts, gradient_parts, zr1, zr2, zr3, xr1, xr2, xr3, yr1, yr2, yr3,
+    zb, zc, xb, xc, yb, yc, pieces, local_sem, core_sem, part_sem, s1, r1, s2, r2, s3, r3, s4, r4,
 ):
     x, y, z, core = place()
 
@@ -137,34 +139,63 @@
         started.append(copy)
         return copy
 
+    def fetch(w):
+        at, size = WINDOWS[w]
+        return [
+            pltpu.make_async_copy(
+                weight.at[pl.ds(at, size), :],
+                weight_parts.at[w % 2, pl.ds(0, size), :],
+                part_sem.at[0, w % 2],
+            ),
+            pltpu.make_async_copy(
+                gradient.at[:, pl.ds(at, size)],
+                gradient_parts.at[w % 2, :, pl.ds(0, size)],
+                part_sem.at[1, w % 2],
+            ),
+        ]
+
+    tokens = moved.shape[0]
+    lanes = pl.ds(pl.multiple_of(core * tokens, 128), tokens)
+    mine_moved = pltpu.make_async_copy(moved, tokens_all.at[lanes, :], local_sem.at[8])
+    mine_moved.start()
+    their_moved = send(
+        moved, tokens_all.at[lanes, :], core_sem.at[0, 8], core_sem.at[1, 8], to(dc=1)
+    )
+    swaps = {}
     order = [(zi, yi) for zi in (1, 3, 2, 0) for yi in (1, 0)]
-    swaps = {}
     for n, (zi, yi) in enumerate(order):
         block = 2 * flip(z, zi) + flip(y, yi) % 2
         mine = pltpu.make_async_copy(
-            product.at[2 * block + core], own.at[zi, yi], local_sem.at[n]
+            gradient_rows.at[2 * block + core], operand.at[zi, yi, :, lanes], local_sem.at[n]
         )
         mine.start()
         theirs = send(
-            product.at[2 * block + 1 - core], other.at[zi, yi],
+            gradient_rows.at[2 * block + 1 - core], operand.at[zi, yi, :, lanes],
             core_sem.at[0, n], core_sem.at[1, n], to(dc=1),
         )
         swaps[zi, yi] = (mine, theirs)
+    windows = [fetch(0), fetch(1)]
+    for pair in windows:
+        for copy in pair:
+            copy.start()
+    mine_moved.wait()
+    their_moved.wait_recv()
 
     first = {"z": [], "x": [], "y": []}
     for zi, yi in order:
-        mine, theirs = swaps[zi, yi]
-        mine.wait()
-        theirs.wait_recv()
-        mine_ref, other_ref = own.at[zi, yi], other.at[zi, yi]
-
-        def keep(at, total, mine_ref=mine_ref):
-            mine_ref[at, :] = total.astype(jnp.bfloat16)
-
-        add_rows(
-            OWN_ROWS, keep,
-            [lambda at, ref=mine_ref: ref[at, :], lambda at, ref=other_ref: ref[at, :]],
-        )
+        if yi:
+            for each in (1, 0):
+                mine, theirs = swaps[zi, each]
+                mine.wait()
+                theirs.wait_recv()
+            rows = operand[zi].reshape(2 * OWN_ROWS, 2 * tokens)
+            for at, size in ((0, 1024), (1024, 896)):
+                term = jnp.dot(
+                    rows, tokens_all[:, at : at + size], preferred_element_type=jnp.float32
+                )
+                own[zi, :, :, at : at + size] = term.astype(jnp.bfloat16).reshape(
+                    2, OWN_ROWS, size
+                )
         if zi:
             n = (zi - 1) * 2 + yi
             first["z"].append(send(
@@ -183,6 +214,23 @@
                 own.at[zi, yi, pl.ds(Y_AT, Y_ROWS), pl.ds(half(flip(y, k)), 1024)],
                 yr1.at[k - 1, zi], s1.at[n], r1.at[n], to(dy=k),
             ))
+
+    for w in range(len(WINDOWS)):
+        for copy in windows[w]:
+            copy.wait()
+        size = WINDOWS[w][1]
+        for at, width in ((0, 1024), (1024, 896)):
+            term = jnp.dot(
+                gradient_parts[w % 2, :, 0:size],
+                weight_parts[w % 2, 0:size, at : at + width],
+                preferred_element_type=jnp.float32,
+            )
+            columns = slice(at, at + width)
+            grad_moved[:, columns] = term if w == 0 else grad_moved[:, columns] + term
+        if w + 2 < len(WINDOWS):
+            windows.append(fetch(w + 2))
+            for copy in windows[w + 2]:
+                copy.start()
 
     def store_to(ref):
         def store(at, total):
@@ -326,11 +374,12 @@
         copy.wait_send()
 
 
-def reduce_blocks(product):
-    features = product.shape[1]
+def reduce_blocks(grad_pre, moved, weight):
+    tokens, features = moved.shape
     bf16 = jnp.bfloat16
     shapes = [
-        (4, 2, OWN_ROWS, features), (4, 2, OWN_ROWS, features),
+        (4, 2, OWN_ROWS, features), (4, 2, OWN_ROWS, 2 * tokens), (2 * tokens, features),
+        (2, 1024, features), (2, tokens, 1024),
         (3, 2, Z_ROWS, features), (3, 2, Z_ROWS, 512), (3, Z_ROWS, 256),
         (3, 4, 2, X_ROWS, 512), (3, 4, X_ROWS, 256), (3, X_ROWS, 256),
         (3, 4, Y_ROWS, 1024), (3, Y_ROWS, 1024), (3, Y_ROWS, 256),
@@ -339,19 +388,22 @@
         (4, Y_ROWS, 1024), (Y_ROWS, 1024),
         (8, OWN_ROWS, 256),
     ]
-    sems = [(8,), (2, 8), (42,), (42,), (9,), (9,), (9,), (9,), (7,), (7,)]
+    sems = [(9,), (2, 9), (2, 2), (42,), (42,), (9,), (9,), (9,), (9,), (7,), (7,)]
     return pl.pallas_call(
         reduce_kernel,
-        out_shape=jax.ShapeDtypeStruct((OWN_ROWS, features), jnp.float32),
-        in_specs=[pl.BlockSpec(memory_space=pl.ANY)],
-        out_specs=pl.BlockSpec(memory_space=pltpu.VMEM),
+        out_shape=(
+            jax.ShapeDtypeStruct((OWN_ROWS, features), jnp.float32),
+            jax.ShapeDtypeStruct((tokens, features), jnp.float32),
+        ),
+        in_specs=[pl.BlockSpec(memory_space=pl.ANY)] * 4,
+        out_specs=[pl.BlockSpec(memory_space=pltpu.VMEM)] * 2,
         scratch_shapes=[pltpu.VMEM(shape, bf16) for shape in shapes]
         + [pltpu.SemaphoreType.DMA(shape) for shape in sems],
         compiler_params=pltpu.CompilerParams(
-            collective_id=0, has_side_effects=True, vmem_limit_bytes=56 << 20
+            collective_id=0, has_side_effects=True, vmem_limit_bytes=60 << 20
         ),
         name="reduce_blocks",
-    )(product.reshape(-1, OWN_ROWS, features))
+    )(grad_pre.T.reshape(-1, OWN_ROWS, tokens), grad_pre, moved, weight)
 
 
 def per_device(tokens, timesteps, table, weight_values, weight_scales, cotangent):
@@ -364,11 +416,7 @@
     gelu_value, derivative = gelu_slope(preact)
     hidden = gelu_value.astype(jnp.bfloat16)
     grad_pre = (upstream * derivative).astype(jnp.bfloat16)
-    grad_moved = jnp.dot(grad_pre, weight, preferred_element_type=jnp.float32)
-    product = lax.dot_general(
-        grad_pre, moved, (((0,), (0,)), ((), ())), preferred_element_type=jnp.float32
-    )
-    grad_weight = reduce_blocks(product.astype(jnp.bfloat16))
+    grad_weight, grad_moved = reduce_blocks(grad_pre, moved, weight)
     grad_tokens = normalize_back(grad_moved, normed, inverse, factor)
     return (hidden, grad_weight, grad_tokens)
 

time: 280 us -> 254 us (0.907)
  matrix products: 66.1 us -> 23.2 us
  local copies, waits for them, and re-layouts: 3.09 us -> 10.5 us
  Pallas kernels: 88.5 us -> 93.7 us
  other arithmetic: 8.95 us -> 12.5 us
    dot_general x2 -> x0, matrix products: 47 us -> none  [the longest x1 23.8 us: per_device(): grad_moved = jnp.dot(grad_pre, weight, preferred_element_type=jnp.float32)]
    transpose x0 -> x1, local copies, waits for them, and re-layouts: none -> 7.55 us  [reduce_blocks(): grad_pre.T.reshape(-1, OWN_ROWS, tokens)]
    pallas_call x1, Pallas kernels: 88.5 us -> 93.7 us  [reduce_blocks(): pl.pallas_call(reduce_kernel, out_shape=(jax.ShapeDtypeStruct((OWN_ROWS,...]
    dot_general x1, matrix products: 18.7 us -> 22.8 us  [per_device(): jnp.einsum('td,fd->tf', moved, weight, preferred_element_type=jnp.float32)]
    reduce_sum x0 -> x1, other arithmetic: none -> 3.44 us  [normalize_back(): mean_grad = jnp.mean(scaled_grad, axis=2, keepdims=True)]
  transfers between devices with their start and end apart: 1 -> 1, of which waited for: 1 -> 1; matrix products, arithmetic and copies ran while one was open for 1% -> 2% of each run, Pallas kernels for 0% -> 0%
where the time goes in v3:
time: 254 us; the launch traced here: 253 us
  waiting for transfers between devices  99.3 us (39%)
  Pallas kernels  93.7 us (37%)
  matrix products  23.2 us (9%)
  between operations  14.1 us (6%)
  other arithmetic  12.5 us (5%)
  local copies, waits for them, and re-layouts  10.5 us (4%)
    all_gather x1, waiting for transfers between devices, per_device(): lax.all_gather(dequantize(weight_values, weight_scales), 'shard', axis=0,...  99.3 us
    pallas_call x1, Pallas kernels, reduce_blocks(): pl.pallas_call(reduce_kernel, out_shape=(jax.ShapeDtypeStruct((OWN_ROWS,...  93.7 us
    dot_general x1, matrix products, per_device(): jnp.einsum('td,fd->tf', moved, weight, preferred_element_type=jnp.float32)  22.8 us
    transpose x1, local copies, waits for them, and re-layouts, reduce_blocks(): grad_pre.T.reshape(-1, OWN_ROWS, tokens)  7.55 us
  transfers between devices with their start and end apart: 1, of which 1 were waited for; matrix products, arithmetic and copies ran while one was open for 2% of the time, Pallas kernels for 0%

profile of v3, /device:TPU:0, one launch (start us, length us, event | category | flops | bytes accessed | tf_op | source)
XLA Modules:
  0.0 253.4 jit_solution(15360563049606662244)
XLA Ops:
  7.2 0.0 all-gather.2.cloned.1.call-start
  7.2 0.8 copy.12
  8.0 0.0 copy-start
  8.1 0.7 mul.124
  8.8 0.0 copy-start.3
  8.8 0.0 copy-start.4
  8.8 3.2 %fusion.19 = bf16[304,1920]{1,0:T(8,128)(2,1)} fusion(f32[38,8,15,128]{3,2,1,0:T(8,128)S(1)} %bitcast.44, bf16[304,1920]{1,0:T(8,128)(2,1)} %param.9), kind=kLoop, calls=%fused_computation.27 | loop fusion | flops 1751040 | bytes 4669440 | tf_op jit(solution)/shard_map/convert_element_type | solution.py:30
  12.0 0.0 all-gather.2.cloned.1.call-update
  12.0 0.0 copy-done
  12.0 0.3 convert_reduce_fusion
  12.3 0.7 fusion.15
  13.0 0.0 copy-done.3
  13.0 0.0 copy-done.4
  13.0 0.4 fusion.20
  13.5 2.5 fusion.17.moved
  15.9 99.3 %all-gather.2.cloned.1.call-done.weight = bf16[4864,1920]{1,0:T(8,128)(2,1)} async-done(((bf16[304,1920]{1,0:T(8,128)(2,1)}), bf16[4864,1920]{1,0:T(8,128)(2,1)}) %all-gather.2.cloned.1.call-update) | async-done | bytes 18677776 | tf_op jit(solution)/shard_map/all_gather | solution.py:412
  115.2 22.8 %fusion.6 = (bf16[512,4864]{1,0:T(8,128)(2,1)}, bf16[512,4864]{1,0:T(8,128)(2,1)}) fusion(bf16[512,4864]{1,0:T(8,128)(2,1)} %param.11, bf16[512,1920]{1,0:T(8,128)(2,1)} %fusion.17.moved, bf16[4864,1920]{1,0:T(8,128)(2,1)} %all-gather.2.cloned.1.call-done.weight), kind=kOutput, calls=%fused_computation.8 | convolution fusion | flops 9617801216 | bytes 35586048 | tf_op jit(solution)/shard_map/td,fd->tf/dot_general | solution.py:415
  138.0 7.6 %copy.13 = bf16[4864,512]{1,0:T(8,128)(2,1)} copy(bf16[4864,512]{0,1:T(8,128)(2,1)} %bitcast.42) | data formatting | bytes 9961472 | tf_op jit(solution)/shard_map/transpose | solution.py:406
  145.6 93.7 %reduce_blocks.1 = (f32[304,1920]{1,0:T(8,128)}, f32[512,1920]{1,0:T(8,128)}) custom-call(bf16[16,304,512]{2,1,0:T(8,128)(2,1)} %bitcast.43, bf16[512,4864]{1,0:T(8,128)(2,1)} %get-tuple-element.9.gradient, bf16[512,1920]{1,0:T(8,128)(2,1)} %fusion.17.moved, bf16[4864,1920]{1,0:T(8,128)(2,1)} %all-gather.2.cloned.1.call-done.weight), custom_call_target="tpu_custom_call" | custom-call | tf_op jit(solution)/shard_map/reduce_blocks/pallas_call | solution.py:392
  239.3 0.0 copy-start.1
  239.3 3.4 %fusion.18 = (f32[512]{0:T(512)S(1)}, f32[512]{0:T(512)S(1)}) fusion(f32[512,1920]{1,0:T(8,128)} %get-tuple-element.6, f32[2,1920]{1,0:T(2,128)S(1)} %get-tuple-element.11, f32[512]{0:T(512)S(1)} %add_rsqrt_fusion, f32[512]{0:T(512)S(1)} %broadcast_multiply_fusion.2, bf16[512,1920]{1,0:T(8,128)(2,1)S(1)} %copy-done), kind=kLoop, calls=%fused_computation.25 | loop fusion | flops 6880256 | bytes 5921792 | tf_op jit(solution)/shard_map/reduce_sum | solution.py:57
  242.7 0.0 copy-done.1
  242.7 0.0 copy-start.2
  242.7 2.4 fusion.14
  245.1 0.0 copy-done.2
  245.1 1.4 copy.26
  (4 shorter events, 0.0 us)
Async XLA Ops:
  7.2 108.1 %all-gather.2.cloned.1.call-start = ((), (), s32[]{:S(2)}) async-start(), calls=%async_computation | async-start | bytes 19845120 | tf_op jit(solution)/shard_map/all_gather | solution.py:412
  8.0 3.9 %copy-start = (bf16[512,1920]{1,0:T(8,128)(2,1)S(1)}, bf16[512,1920]{1,0:T(8,128)(2,1)}, u32[]{:S(2)}) copy-start(bf16[512,1920]{1,0:T(8,128)(2,1)} %param.6) | copy-start | bytes 5898244
  8.8 4.2 %copy-start.3 = (f32[64,2,1920]{2,1,0:T(2,128)S(1)}, f32[64,2,1920]{2,1,0:T(2,128)}, u32[]{:S(2)}) copy-start(f32[64,2,1920]{2,1,0:T(2,128)} %param.8) | copy-start | bytes 2949124
  8.8 4.2 %copy-start.4 = (s32[2]{0:T(128)S(1)}, s32[2]{0:T(128)}, u32[]{:S(2)}) copy-start(s32[2]{0:T(128)} %param.7) | copy-start | bytes 28
  239.3 3.5 %copy-start.1 = (f32[512,1920]{1,0:T(8,128)S(1)}, f32[512,1920]{1,0:T(8,128)}, u32[]{:S(2)}) copy-start(f32[512,1920]{1,0:T(8,128)} %get-tuple-element.6) | copy-start | bytes 11796484
  242.7 2.4 copy-start.2
Sparse Core Ops, SparseCore 0:
  12.1 103.0 all-gather.1

commit v4 on v3

--- a/solution.py
+++ b/solution.py
@@ -47,17 +47,7 @@
     normed = centre * inverse
     factor = 1.0 + picked[:, 1][:, None, :]
     moved = (normed * factor + picked[:, 0][:, None, :]).reshape(-1, features).astype(jnp.bfloat16)
-    return (moved, normed, inverse, factor)
-
-
-def normalize_back(grad_moved, normed, inverse, factor):
-    samples = normed.shape[0]
-    features = normed.shape[2]
-    scaled_grad = grad_moved.reshape(samples, -1, features) * factor
-    mean_grad = jnp.mean(scaled_grad, axis=2, keepdims=True)
-    mean_prod = jnp.mean(scaled_grad * normed, axis=2, keepdims=True)
-    result = inverse * (scaled_grad - mean_grad - normed * mean_prod)
-    return result.reshape(-1, features).astype(jnp.bfloat16)
+    return (moved, factor)
 
 
 MESH = pl.DeviceIdType.MESH
@@ -111,7 +101,7 @@
 
 
 def reduce_kernel(
-    gradient_rows, gradient, moved, weight, out, grad_moved, own, operand, tokens_all,
+    gradient_rows, gradient, moved, weight, tokens, factor, out, grad_tokens, grad_moved, own, operand, tokens_all,
     weight_parts, gradient_parts, zr1, zr2, zr3, xr1, xr2, xr3, yr1, yr2, yr3,
     zb, zc, xb, xc, yb, yc, pieces, local_sem, core_sem, part_sem, s1, r1, s2, r2, s3, r3, s4, r4,
 ):
@@ -122,7 +112,6 @@
 
     peers = [to(dc=1)]
     peers += [to(dx=k) for k in KS] + [to(dy=k) for k in KS] + [to(dz=k) for k in KS]
-    peers += [to(dx=k, dy=2) for k in KS]
     barrier = pltpu.get_barrier_semaphore()
     for peer in peers:
         pl.semaphore_signal(barrier, inc=1, device_id=peer, device_id_type=MESH)
@@ -154,8 +143,8 @@
             ),
         ]
 
-    tokens = moved.shape[0]
-    lanes = pl.ds(pl.multiple_of(core * tokens, 128), tokens)
+    count = moved.shape[0]
+    lanes = pl.ds(pl.multiple_of(core * count, 128), count)
     mine_moved = pltpu.make_async_copy(moved, tokens_all.at[lanes, :], local_sem.at[8])
     mine_moved.start()
     their_moved = send(
@@ -188,7 +177,7 @@
                 mine, theirs = swaps[zi, each]
                 mine.wait()
                 theirs.wait_recv()
-            rows = operand[zi].reshape(2 * OWN_ROWS, 2 * tokens)
+            rows = operand[zi].reshape(2 * OWN_ROWS, 2 * count)
             for at, size in ((0, 1024), (1024, 896)):
                 term = jnp.dot(
                     rows, tokens_all[:, at : at + size], preferred_element_type=jnp.float32
@@ -285,6 +274,23 @@
                 s2.at[5 + k], r2.at[5 + k], to(dy=k),
             ))
 
+    per_sample = count // factor.shape[0]
+
+    def finish(step, _):
+        at = pl.ds(pl.multiple_of(step * 16, 16), 16)
+        value = tokens[at, :].astype(jnp.float32)
+        centre = value - jnp.mean(value, axis=1, keepdims=True)
+        inverse = lax.rsqrt(jnp.mean(centre * centre, axis=1, keepdims=True) + epsilon)
+        normed = centre * inverse
+        scaled_grad = grad_moved[at, :] * factor[pl.ds(step * 16 // per_sample, 1), :]
+        mean_grad = jnp.mean(scaled_grad, axis=1, keepdims=True)
+        mean_prod = jnp.mean(scaled_grad * normed, axis=1, keepdims=True)
+        result = inverse * (scaled_grad - mean_grad - normed * mean_prod)
+        grad_tokens[at, :] = result.astype(jnp.bfloat16)
+        return 0
+
+    lax.fori_loop(0, count // 16, finish, 0)
+
     third = {"z": [], "x": [], "y": []}
     for copy in second["z"]:
         copy.wait_recv()
@@ -346,15 +352,17 @@
         X_ROWS, store_piece(X_AT), [plain(xc.at[0])] + [plain(xr3.at[k - 1]) for k in KS]
     )
 
-    spread = []
-    for dx in (0, 1, 3, 2):
-        for dy in (2, 0):
-            if dx or dy:
-                n = 2 * dx + dy // 2
-                spread.append(send(
-                    pieces.at[0], pieces.at[n], s4.at[n - 1], r4.at[n - 1], to(dx=dx, dy=dy)
-                ))
-    for copy in spread:
+    def hand(source, slot, peer):
+        return send(
+            pieces.at[source], pieces.at[slot], s4.at[slot - 1], r4.at[slot - 1], peer
+        )
+
+    along = {k: hand(0, 2 * k, to(dx=k)) for k in KS}
+    across = [hand(0, 1, to(dy=2))]
+    for k in KS:
+        along[k].wait_recv()
+        across.append(hand(2 * k, 2 * k + 1, to(dy=2)))
+    for copy in across:
         copy.wait_recv()
     for px in range(4):
         for ph in range(2):
@@ -374,12 +382,12 @@
         copy.wait_send()
 
 
-def reduce_blocks(grad_pre, moved, weight):
-    tokens, features = moved.shape
+def reduce_blocks(grad_pre, moved, weight, tokens, factor):
+    count, features = moved.shape
     bf16 = jnp.bfloat16
     shapes = [
-        (4, 2, OWN_ROWS, features), (4, 2, OWN_ROWS, 2 * tokens), (2 * tokens, features),
-        (2, 1024, features), (2, tokens, 1024),
+        (4, 2, OWN_ROWS, features), (4, 2, OWN_ROWS, 2 * count), (2 * count, features),
+        (2, 1024, features), (2, count, 1024),
         (3, 2, Z_ROWS, features), (3, 2, Z_ROWS, 512), (3, Z_ROWS, 256),
         (3, 4, 2, X_ROWS, 512), (3, 4, X_ROWS, 256), (3, X_ROWS, 256),
         (3, 4, Y_ROWS, 1024), (3, Y_ROWS, 1024), (3, Y_ROWS, 256),
@@ -393,31 +401,168 @@
         reduce_kernel,
         out_shape=(
             jax.ShapeDtypeStruct((OWN_ROWS, features), jnp.float32),
-            jax.ShapeDtypeStruct((tokens, features), jnp.float32),
+            jax.ShapeDtypeStruct((count, features), bf16),
         ),
-        in_specs=[pl.BlockSpec(memory_space=pl.ANY)] * 4,
+        in_specs=[pl.BlockSpec(memory_space=pl.ANY)] * 4
+        + [pl.BlockSpec(memory_space=pltpu.VMEM)] * 2,
         out_specs=[pl.BlockSpec(memory_space=pltpu.VMEM)] * 2,
-        scratch_shapes=[pltpu.VMEM(shape, bf16) for shape in shapes]
+        scratch_shapes=[pltpu.VMEM((count, features), jnp.float32)]
+        + [pltpu.VMEM(shape, bf16) for shape in shapes]
         + [pltpu.SemaphoreType.DMA(shape) for shape in sems],
         compiler_params=pltpu.CompilerParams(
             collective_id=0, has_side_effects=True, vmem_limit_bytes=60 << 20
         ),
         name="reduce_blocks",
-    )(grad_pre.T.reshape(-1, OWN_ROWS, tokens), grad_pre, moved, weight)
+    )(grad_pre.T.reshape(-1, OWN_ROWS, count), grad_pre, moved, weight, tokens, factor)
+
+
+GX_ROWS, GZ_ROWS, GY_ROWS = 128, 32, 144
+GX_PART = GX_ROWS // 4
+GY_AT = GX_ROWS + GZ_ROWS
+HALVES = {1: (0, 1024), 3: (1024, 896)}
+
+
+def gather_kernel(mine, whole, own_sem, ss, rs):
+    x, y, z, core = place()
+
+    def to(dx=0, dy=0, dz=0, dc=0):
+        return device_at(flip(x, dx), flip(y, dy), flip(z, dz), 1 - core if dc else core)
+
+    peers = [to(dc=1)]
+    peers += [to(dx=k) for k in KS] + [to(dy=k) for k in (1, 3)] + [to(dz=k) for k in KS]
+    barrier = pltpu.get_barrier_semaphore()
+    for peer in peers:
+        pl.semaphore_signal(barrier, inc=1, device_id=peer, device_id_type=MESH)
+    pl.semaphore_wait(barrier, len(peers))
+
+    started, shared = [], []
+
+    def send(source, block, rows, columns, peer):
+        n = len(started)
+        copy = pltpu.make_async_remote_copy(
+            src_ref=source.at[rows, columns],
+            dst_ref=whole.at[block, rows, columns],
+            send_sem=ss.at[n], recv_sem=rs.at[n],
+            device_id=peer, device_id_type=MESH,
+        )
+        copy.start()
+        started.append(copy)
+        return copy
+
+    every = slice(None)
+
+    def block_of(zi, yi):
+        return 2 * (2 * flip(z, zi) + flip(y, yi) % 2) + core
+
+    own = block_of(0, 0)
+    keep = pltpu.make_async_copy(mine, whole.at[own], own_sem)
+    keep.start()
+
+    def share(source, block, rows, columns):
+        shared.append(send(source, block, rows, columns, to(dc=1)))
+
+    xpart = pl.ds(pl.multiple_of(GX_PART * x, 8), GX_PART)
+    zrows, yrows, zyrows = pl.ds(GX_ROWS, GZ_ROWS), pl.ds(GY_AT, GY_ROWS), pl.ds(GX_ROWS, GZ_ROWS + GY_ROWS)
+    cols = {k: pl.ds(*HALVES[k]) for k in HALVES}
+
+    xz, xy, xx, zyz, yy, zy, zz = {}, {}, {}, {}, {}, {}, {}
+
+    def x_down(zi, yi, source):
+        for k in KS:
+            xx[zi, yi, k] = send(source, block_of(zi, yi), xpart, every, to(dx=k))
+
+    def x_across(zi, source):
+        for k in (1, 3):
+            xy[zi, k] = send(source, block_of(zi, 0), xpart, cols[k], to(dy=k))
+
+    def y_across(zi, source):
+        for k in (1, 3):
+            yy[zi, k] = send(source, block_of(zi, 0), yrows, cols[k], to(dy=k))
+
+    for k in KS:
+        xz[k] = send(mine, own, xpart, every, to(dz=k))
+    x_across(0, mine)
+    zyz[1] = send(mine, own, zyrows, every, to(dz=1))
+    for k in (1, 3):
+        zy[k] = send(mine, own, zrows, cols[k], to(dy=k))
+    y_across(0, mine)
+    zyz[3] = send(mine, own, zyrows, every, to(dz=3))
+    zyz[2] = send(mine, own, zyrows, every, to(dz=2))
+    share(mine, own, every, every)
+
+    for zi in KS:
+        xz[zi].wait_recv()
+        source = whole.at[block_of(zi, 0)]
+        x_across(zi, source)
+        x_down(zi, 0, source)
+        share(source, block_of(zi, 0), xpart, every)
+    for zi in (0, 1, 3, 2):
+        for k in (1, 3):
+            xy[zi, k].wait_recv()
+        source = whole.at[block_of(zi, 1)]
+        x_down(zi, 1, source)
+        share(source, block_of(zi, 1), xpart, every)
+    for k in (1, 3):
+        zy[k].wait_recv()
+    source = whole.at[block_of(0, 1)]
+    for k in KS:
+        zz[k] = send(source, block_of(0, 1), zrows, every, to(dz=k))
+    share(source, block_of(0, 1), zrows, every)
+    for zi in KS:
+        zyz[zi].wait_recv()
+        source = whole.at[block_of(zi, 0)]
+        y_across(zi, source)
+        share(source, block_of(zi, 0), zyrows, every)
+    for zi in (0, 1, 3, 2):
+        for k in (1, 3):
+            yy[zi, k].wait_recv()
+        share(whole.at[block_of(zi, 1)], block_of(zi, 1), yrows, every)
+    for zi in KS:
+        zz[zi].wait_recv()
+        share(whole.at[block_of(zi, 1)], block_of(zi, 1), zrows, every)
+    for yi in (0, 1):
+        for zi in (0, 1, 3, 2):
+            for k in KS if zi or yi else ():
+                xx[zi, yi, k].wait_recv()
+                rows = pl.ds(pl.multiple_of(GX_PART * flip(x, k), 8), GX_PART)
+                share(whole.at[block_of(zi, yi)], block_of(zi, yi), rows, every)
+    keep.wait()
+    for copy in shared:
+        copy.wait_recv()
+    for copy in started:
+        copy.wait_send()
+
+
+def gather_blocks(mine):
+    rows, features = mine.shape
+    copies = 120
+    whole = pl.pallas_call(
+        gather_kernel,
+        out_shape=jax.ShapeDtypeStruct((16, rows, features), mine.dtype),
+        in_specs=[pl.BlockSpec(memory_space=pl.ANY)],
+        out_specs=pl.BlockSpec(memory_space=pl.ANY),
+        scratch_shapes=[
+            pltpu.SemaphoreType.DMA(()),
+            pltpu.SemaphoreType.DMA((copies,)),
+            pltpu.SemaphoreType.DMA((copies,)),
+        ],
+        compiler_params=pltpu.CompilerParams(collective_id=1, has_side_effects=True),
+        name="gather_blocks",
+    )(mine)
+    return whole.reshape(16 * rows, features)
 
 
 def per_device(tokens, timesteps, table, weight_values, weight_scales, cotangent):
-    moved, normed, inverse, factor = modulate(tokens, timesteps, table)
+    moved, factor = modulate(tokens, timesteps, table)
     upstream = cotangent.astype(jnp.float32)
-    weight = lax.all_gather(
-        dequantize(weight_values, weight_scales), "shard", axis=0, tiled=True
-    )
+    weight = gather_blocks(dequantize(weight_values, weight_scales))
     preact = jnp.einsum("td,fd->tf", moved, weight, preferred_element_type=jnp.float32)
     gelu_value, derivative = gelu_slope(preact)
     hidden = gelu_value.astype(jnp.bfloat16)
     grad_pre = (upstream * derivative).astype(jnp.bfloat16)
-    grad_weight, grad_moved = reduce_blocks(grad_pre, moved, weight)
-    grad_tokens = normalize_back(grad_moved, normed, inverse, factor)
+    grad_weight, grad_tokens = reduce_blocks(
+        grad_pre, moved, weight, tokens, factor.reshape(factor.shape[0], -1)
+    )
     return (hidden, grad_weight, grad_tokens)
 
 

time: 254 us -> 199 us (0.78)
  waiting for transfers between devices: 99.3 us -> 0 us
  Pallas kernels: 93.7 us -> 153 us
  between operations: 14.1 us -> 0.74 us
  other arithmetic: 12.5 us -> 8.7 us
    all_gather x1 -> x0, waiting for transfers between devices: 99.3 us -> none  [per_device(): lax.all_gather(dequantize(weight_values, weight_scales), 'shard', axis=0,...]
    pallas_call x0 -> x1, Pallas kernels: none -> 62 us  [gather_blocks(): pl.pallas_call(gather_kernel, out_shape=jax.ShapeDtypeStruct((16, rows, f...]
    reduce_sum x1 -> x0, other arithmetic: 3.44 us -> none  [normalize_back(): mean_grad = jnp.mean(scaled_grad, axis=2, keepdims=True)]
    unnamed x11 -> x14, local copies, waits for them, and re-layouts: 1.42 us -> 4.64 us
    pallas_call x1, Pallas kernels: 93.7 us -> 90.5 us  [reduce_blocks(): pl.pallas_call(reduce_kernel, out_shape=(jax.ShapeDtypeStruct((OWN_ROWS,...]
  transfers between devices with their start and end apart: 1 -> 0, of which waited for: 1 -> 0; matrix products, arithmetic and copies ran while one was open for 2% -> 0% of each run, Pallas kernels for 0% -> 0%
where the time goes in v4:
time: 199 us
  Pallas kernels  153 us (77%)
  matrix products  23.8 us (12%)
  local copies, waits for them, and re-layouts  13 us (7%)
  other arithmetic  8.7 us (4%)
    pallas_call x1, Pallas kernels, reduce_blocks(): pl.pallas_call(reduce_kernel, out_shape=(jax.ShapeDtypeStruct((OWN_ROWS,...  90.5 us
    pallas_call x1, Pallas kernels, gather_blocks(): pl.pallas_call(gather_kernel, out_shape=jax.ShapeDtypeStruct((16, rows, f...  62 us
    dot_general x1, matrix products, per_device(): jnp.einsum('td,fd->tf', moved, weight, preferred_element_type=jnp.float32)  22.2 us
    transpose x1, local copies, waits for them, and re-layouts, reduce_blocks(): grad_pre.T.reshape(-1, OWN_ROWS, count)  7.56 us
    unnamed x14, local copies, waits for them, and re-layouts  4.64 us

profile of v4, /device:TPU:0, one launch (start us, length us, event | category | flops | bytes accessed | tf_op | source)
XLA Modules:
  0.0 198.8 jit_solution(14293517794734957920)
XLA Ops:
  0.6 0.0 copy-start
  0.6 0.0 copy-start.5
  0.7 2.0 %convert_reduce_fusion = f32[512]{0:T(512)S(1)} fusion(bf16[512,1920]{1,0:T(8,128)(2,1)} %tokens.1), kind=kLoop, calls=%fused_computation.11 | loop fusion | flops 1965568 | bytes 1968128 | tf_op jit(solution)/shard_map/reduce_sum | solution.py:45
  2.7 0.0 copy-start.3
  2.7 2.3 %fusion.9 = f32[512]{0:T(512)S(1)} fusion(bf16[512,1920]{1,0:T(8,128)(2,1)} %tokens.1, f32[512]{0:T(512)S(1)} %broadcast_multiply_fusion), kind=kLoop, calls=%fused_computation.14 | loop fusion | flops 3931648 | bytes 1970176 | tf_op jit(solution)/shard_map/reduce_sum | solution.py:46
  5.0 1.7 fusion.14
  6.7 0.0 copy-start.4
  6.7 0.0 copy-done.5
  6.7 0.1 copy.12
  6.8 0.0 copy-done
  6.8 2.5 %fusion.12.moved = bf16[512,1920]{1,0:T(8,128)(2,1)} fusion(bf16[512,1920]{1,0:T(8,128)(2,1)S(1)} %copy-done, f32[2,1920]{1,0:T(2,128)S(1)} %get-tuple-element.10, f32[2,1920]{1,0:T(2,128)S(1)} %get-tuple-element.9.factor, f32[512]{0:T(512)S(1)} %add_rsqrt_fusion, f32[512]{0:T(512)S(1)} %broadcast_multiply_fusion), kind=kLoop, calls=%fused_computation.17 | loop fusion | flops 5898240 | bytes 3966976 | tf_op jit(solution)/shard_map/convert_element_type | solution.py:49
  9.3 0.7 mul.93
  10.0 0.0 copy-done.3
  10.0 1.9 fusion.13.mine
  11.9 0.0 copy-done.4
  11.9 0.0 copy-start.1
  11.9 62.0 %gather_blocks.1 = bf16[16,304,1920]{2,1,0:T(8,128)(2,1)} custom-call(bf16[304,1920]{1,0:T(8,128)(2,1)} %fusion.13.mine), custom_call_target="tpu_custom_call" | custom-call | tf_op jit(solution)/shard_map/gather_blocks/pallas_call | solution.py:539
  73.9 0.0 copy-done.1
  73.9 22.2 %fusion.6 = (bf16[512,4864]{1,0:T(8,128)(2,1)}, bf16[512,4864]{1,0:T(8,128)(2,1)}) fusion(bf16[512,4864]{1,0:T(8,128)(2,1)} %param.11, bf16[512,1920]{1,0:T(8,128)(2,1)S(1)} %copy-done.1, bf16[4864,1920]{1,0:T(8,128)(2,1)} %bitcast.32), kind=kOutput, calls=%fused_computation.8 | convolution fusion | flops 9617801216 | bytes 35586048 | tf_op jit(solution)/shard_map/td,fd->tf/dot_general | solution.py:559
  96.0 7.6 %copy.13 = bf16[4864,512]{1,0:T(8,128)(2,1)} copy(bf16[4864,512]{0,1:T(8,128)(2,1)} %bitcast.34) | data formatting | bytes 9961472 | tf_op jit(solution)/shard_map/transpose | solution.py:416
  103.6 90.5 %reduce_blocks.1 = (f32[304,1920]{1,0:T(8,128)}, bf16[512,1920]{1,0:T(8,128)(2,1)}) custom-call(bf16[16,304,512]{2,1,0:T(8,128)(2,1)} %bitcast.35, bf16[512,4864]{1,0:T(8,128)(2,1)} %get-tuple-element.7.gradient, bf16[512,1920]{1,0:T(8,128)(2,1)} %fusion.12.moved, bf16[4864,1920]{1,0:T(8,128)(2,1)} %bitcast.33, bf16[512,1920]{1,0:T(8,128)(2,1)} %tokens.1, ...), custom_call_target="tpu_custom_call" | custom-call | tf_op jit(solution)/shard_map/reduce_blocks/pallas_call | solution.py:400
  194.2 0.0 copy-start.2
  194.2 3.3 %copy.27 = f32[304,1920]{1,0:T(8,128)} copy(f32[304,1920]{1,0:T(8,128)} %get-tuple-element.15) | data formatting | bytes 4669440
  197.5 0.0 copy-done.2
  197.5 1.3 copy.28
  (3 shorter events, 0.0 us)
Async XLA Ops:
  0.6 6.2 %copy-start = (bf16[512,1920]{1,0:T(8,128)(2,1)S(1)}, bf16[512,1920]{1,0:T(8,128)(2,1)}, u32[]{:S(2)}) copy-start(bf16[512,1920]{1,0:T(8,128)(2,1)} %tokens.1) | copy-start | bytes 5898244
  0.6 6.0 %copy-start.5 = (bf16[304,15]{0,1:T(8,128)(2,1)S(1)}, bf16[304,15]{0,1:T(8,128)(2,1)}, u32[]{:S(2)}) copy-start(bf16[304,15]{0,1:T(8,128)(2,1)} %param.10) | copy-start | bytes 27364
  2.7 7.3 %copy-start.3 = (bf16[304,1920]{1,0:T(8,128)(2,1)S(1)}, bf16[304,1920]{1,0:T(8,128)(2,1)}, u32[]{:S(2)}) copy-start(bf16[304,1920]{1,0:T(8,128)(2,1)} %param.9) | copy-start | bytes 3502084
  6.7 5.2 %copy-start.4 = (f32[2,1920]{1,0:T(2,128)}, f32[2,1920]{1,0:T(2,128)S(1)}, u32[]{:S(2)}) copy-start(f32[2,1920]{1,0:T(2,128)S(1)} %get-tuple-element.9.factor) | copy-start | bytes 46084
  11.9 62.0 %copy-start.1 = (bf16[512,1920]{1,0:T(8,128)(2,1)S(1)}, bf16[512,1920]{1,0:T(8,128)(2,1)}, u32[]{:S(2)}) copy-start(bf16[512,1920]{1,0:T(8,128)(2,1)} %fusion.12.moved) | copy-start | bytes 5898244
  194.2 3.4 %copy-start.2 = (bf16[512,1920]{1,0:T(8,128)(2,1)S(1)}, bf16[512,1920]{1,0:T(8,128)(2,1)}, u32[]{:S(2)}) copy-start(bf16[512,1920]{1,0:T(8,128)(2,1)} %get-tuple-element.16) | copy-start | bytes 5898244

commit v5 on v4

--- a/solution.py
+++ b/solution.py
@@ -30,24 +30,15 @@
     return expanded.reshape(row_count, features).astype(jnp.bfloat16)
 
 
-def modulate(tokens, timesteps, table):
-    samples = timesteps.shape[0]
-    step_count = table.shape[0]
-    features = tokens.shape[1]
+def pick(timesteps, table):
+    step_count, _, features = table.shape
     onehot = (timesteps[:, None] == jnp.arange(step_count, dtype=jnp.int32)[None, :]).astype(
         jnp.float32
     )
     picked = jnp.dot(
         onehot, table.reshape(step_count, 2 * features), precision=lax.Precision.HIGHEST
     )
-    picked = picked.reshape(samples, 2, features)
-    grouped = tokens.astype(jnp.float32).reshape(samples, -1, features)
-    centre = grouped - jnp.mean(grouped, axis=2, keepdims=True)
-    inverse = lax.rsqrt(jnp.mean(centre * centre, axis=2, keepdims=True) + epsilon)
-    normed = centre * inverse
-    factor = 1.0 + picked[:, 1][:, None, :]
-    moved = (normed * factor + picked[:, 0][:, None, :]).reshape(-1, features).astype(jnp.bfloat16)
-    return (moved, factor)
+    return picked[:, :features], 1.0 + picked[:, features:]
 
 
 MESH = pl.DeviceIdType.MESH
@@ -382,7 +373,7 @@
         copy.wait_send()
 
 
-def reduce_blocks(grad_pre, moved, weight, tokens, factor):
+def reduce_blocks(gradient_rows, grad_pre, moved, weight, tokens, factor):
     count, features = moved.shape
     bf16 = jnp.bfloat16
     shapes = [
@@ -413,16 +404,24 @@
             collective_id=0, has_side_effects=True, vmem_limit_bytes=60 << 20
         ),
         name="reduce_blocks",
-    )(grad_pre.T.reshape(-1, OWN_ROWS, count), grad_pre, moved, weight, tokens, factor)
+    )(gradient_rows.reshape(-1, OWN_ROWS, count), grad_pre, moved, weight, tokens, factor)
 
 
 GX_ROWS, GZ_ROWS, GY_ROWS = 128, 32, 144
 GX_PART = GX_ROWS // 4
 GY_AT = GX_ROWS + GZ_ROWS
 HALVES = {1: (0, 1024), 3: (1024, 896)}
-
-
-def gather_kernel(mine, whole, own_sem, ss, rs):
+TILE = 128
+NEAR, FAR = 9, 10
+CHUNK = 256
+
+
+def forward_kernel(
+    mine, tokens, shift, factor, cotangent,
+    whole_out, hidden, gradient, gradient_rows, moved,
+    whole, upstream, hidden_part, gradient_part, rows_part,
+    own_sem, ss, rs, up_sem, out_sem, whole_sem,
+):
     x, y, z, core = place()
 
     def to(dx=0, dy=0, dz=0, dc=0):
@@ -435,13 +434,27 @@
         pl.semaphore_signal(barrier, inc=1, device_id=peer, device_id_type=MESH)
     pl.semaphore_wait(barrier, len(peers))
 
-    started, shared = [], []
-
-    def send(source, block, rows, columns, peer):
+    started = []
+
+    def block_of(zi, yi):
+        return 2 * (2 * flip(z, zi) + flip(y, yi) % 2) + core
+
+    blocks = {(zi, yi): block_of(zi, yi) for zi in range(4) for yi in (0, 1)}
+    own = blocks[0, 0]
+    height = mine.shape[0]
+
+    def within(block, rows):
+        return pl.ds(pl.multiple_of(height * block + rows[0], 16), rows[1])
+
+    def send(block, rows, columns, peer):
         n = len(started)
+        if block is own:
+            source = mine.at[pl.ds(*rows), columns]
+        else:
+            source = whole.at[within(block, rows), columns]
         copy = pltpu.make_async_remote_copy(
-            src_ref=source.at[rows, columns],
-            dst_ref=whole.at[block, rows, columns],
+            src_ref=source,
+            dst_ref=whole.at[within(block, rows), columns],
             send_sem=ss.at[n], recv_sem=rs.at[n],
             device_id=peer, device_id_type=MESH,
         )
@@ -450,118 +463,236 @@
         return copy
 
     every = slice(None)
-
-    def block_of(zi, yi):
-        return 2 * (2 * flip(z, zi) + flip(y, yi) % 2) + core
-
-    own = block_of(0, 0)
-    keep = pltpu.make_async_copy(mine, whole.at[own], own_sem)
+    keep = pltpu.make_async_copy(mine, whole.at[within(own, (0, height)), :], own_sem)
     keep.start()
-
-    def share(source, block, rows, columns):
-        shared.append(send(source, block, rows, columns, to(dc=1)))
-
-    xpart = pl.ds(pl.multiple_of(GX_PART * x, 8), GX_PART)
-    zrows, yrows, zyrows = pl.ds(GX_ROWS, GZ_ROWS), pl.ds(GY_AT, GY_ROWS), pl.ds(GX_ROWS, GZ_ROWS + GY_ROWS)
+    shared = {0: [], 1: [], 3: [], 2: []}
+
+    def share(zi, yi, rows):
+        shared[zi].append(send(blocks[zi, yi], rows, every, to(dc=1)))
+
+    xpart = (GX_PART * x, GX_PART)
+    zrows, yrows = (GX_ROWS, GZ_ROWS), (GY_AT, GY_ROWS)
+    zyrows = (GX_ROWS, GZ_ROWS + GY_ROWS)
     cols = {k: pl.ds(*HALVES[k]) for k in HALVES}
-
     xz, xy, xx, zyz, yy, zy, zz = {}, {}, {}, {}, {}, {}, {}
 
-    def x_down(zi, yi, source):
+    def x_down(zi, yi):
         for k in KS:
-            xx[zi, yi, k] = send(source, block_of(zi, yi), xpart, every, to(dx=k))
-
-    def x_across(zi, source):
+            xx[zi, yi, k] = send(blocks[zi, yi], xpart, every, to(dx=k))
+        share(zi, yi, xpart)
+
+    def x_across(zi):
         for k in (1, 3):
-            xy[zi, k] = send(source, block_of(zi, 0), xpart, cols[k], to(dy=k))
-
-    def y_across(zi, source):
+            xy[zi, k] = send(blocks[zi, 0], xpart, cols[k], to(dy=k))
+
+    def y_across(zi):
         for k in (1, 3):
-            yy[zi, k] = send(source, block_of(zi, 0), yrows, cols[k], to(dy=k))
+            yy[zi, k] = send(blocks[zi, 0], yrows, cols[k], to(dy=k))
+
+    def received(*copies):
+        for copy in copies:
+            copy.wait_recv()
 
     for k in KS:
-        xz[k] = send(mine, own, xpart, every, to(dz=k))
-    x_across(0, mine)
-    zyz[1] = send(mine, own, zyrows, every, to(dz=1))
+        xz[k] = send(own, xpart, every, to(dz=k))
+    x_across(0)
     for k in (1, 3):
-        zy[k] = send(mine, own, zrows, cols[k], to(dy=k))
-    y_across(0, mine)
-    zyz[3] = send(mine, own, zyrows, every, to(dz=3))
-    zyz[2] = send(mine, own, zyrows, every, to(dz=2))
-    share(mine, own, every, every)
-
+        zy[k] = send(own, zrows, cols[k], to(dy=k))
+    zyz[1] = send(own, zyrows, every, to(dz=1))
+    share(0, 0, (0, height))
     for zi in KS:
-        xz[zi].wait_recv()
-        source = whole.at[block_of(zi, 0)]
-        x_across(zi, source)
-        x_down(zi, 0, source)
-        share(source, block_of(zi, 0), xpart, every)
-    for zi in (0, 1, 3, 2):
-        for k in (1, 3):
-            xy[zi, k].wait_recv()
-        source = whole.at[block_of(zi, 1)]
-        x_down(zi, 1, source)
-        share(source, block_of(zi, 1), xpart, every)
-    for k in (1, 3):
-        zy[k].wait_recv()
-    source = whole.at[block_of(0, 1)]
-    for k in KS:
-        zz[k] = send(source, block_of(0, 1), zrows, every, to(dz=k))
-    share(source, block_of(0, 1), zrows, every)
+        received(xz[zi])
+        x_across(zi)
+    y_across(0)
+    received(xy[0, 1], xy[0, 3])
+    x_down(0, 1)
+    received(zy[1], zy[3])
+    zz[1] = send(blocks[0, 1], zrows, every, to(dz=1))
+    share(0, 1, zrows)
+    for k in (3, 2):
+        zyz[k] = send(own, zyrows, every, to(dz=k))
+        zz[k] = send(blocks[0, 1], zrows, every, to(dz=k))
     for zi in KS:
-        zyz[zi].wait_recv()
-        source = whole.at[block_of(zi, 0)]
-        y_across(zi, source)
-        share(source, block_of(zi, 0), zyrows, every)
-    for zi in (0, 1, 3, 2):
-        for k in (1, 3):
-            yy[zi, k].wait_recv()
-        share(whole.at[block_of(zi, 1)], block_of(zi, 1), yrows, every)
-    for zi in KS:
-        zz[zi].wait_recv()
-        share(whole.at[block_of(zi, 1)], block_of(zi, 1), zrows, every)
-    for yi in (0, 1):
-        for zi in (0, 1, 3, 2):
+        x_down(zi, 0)
+        received(xy[zi, 1], xy[zi, 3])
+        x_down(zi, 1)
+
+    count = tokens.shape[0]
+    per_sample = count // factor.shape[0]
+
+    def normalize(step, _):
+        at = pl.ds(pl.multiple_of(step * 16, 16), 16)
+        value = tokens[at, :].astype(jnp.float32)
+        centre = value - jnp.mean(value, axis=1, keepdims=True)
+        inverse = lax.rsqrt(jnp.mean(centre * centre, axis=1, keepdims=True) + epsilon)
+        sample = pl.ds(step * 16 // per_sample, 1)
+        moved[at, :] = (centre * inverse * factor[sample, :] + shift[sample, :]).astype(
+            jnp.bfloat16
+        )
+        return 0
+
+    lax.fori_loop(0, count // 16, normalize, 0)
+
+    low = z % 2
+    plan = []
+    for zi, tiles in ((0, NEAR), (1, FAR), (3, NEAR), (2, FAR)):
+        high = flip(z, zi) % 2
+        first = 19 * (flip(z, zi) // 2) + high * (19 - tiles)
+        plan.append((zi, tiles * TILE, pl.multiple_of(first * TILE, TILE)))
+
+    def fetch(n):
+        zi, size, at = plan[n]
+        copy = pltpu.make_async_copy(
+            cotangent.at[:, pl.ds(at, size)],
+            upstream.at[n % 2, :, pl.ds(0, size)],
+            up_sem.at[n % 2],
+        )
+        copy.start()
+        return copy
+
+    fetched = [fetch(0), fetch(1)]
+    stores = []
+    saved = []
+
+    def window(n):
+        zi, size, at = plan[n]
+        slot = n % 2
+        fetched[n].wait()
+        if n >= 2:
+            for copy in stores[n - 2]:
+                copy.wait()
+
+        def piece(begin, width):
+            values = whole[pl.ds(pl.multiple_of(at + begin, TILE), width), :]
+            preact = lax.dot_general(
+                moved[...], values, (((1,), (1,)), ((), ())),
+                preferred_element_type=jnp.float32,
+            )
+            gelu_value, derivative = gelu_slope(preact)
+            columns = pl.ds(begin, width)
+            hidden_part[slot, :, columns] = gelu_value.astype(jnp.bfloat16)
+            grad = (upstream[slot, :, columns].astype(jnp.float32) * derivative).astype(
+                jnp.bfloat16
+            )
+            gradient_part[slot, :, columns] = grad
+            rows_part[slot, columns, :] = grad.T
+
+        def step(i, _):
+            piece(pl.multiple_of(i * CHUNK, CHUNK), CHUNK)
+            return 0
+
+        lax.fori_loop(0, size // CHUNK, step, 0)
+        if size % CHUNK:
+            piece(size - size % CHUNK, size % CHUNK)
+        target = pl.ds(at, size)
+        copies = [
+            pltpu.make_async_copy(
+                hidden_part.at[slot, :, pl.ds(0, size)], hidden.at[:, target], out_sem.at[0, slot]
+            ),
+            pltpu.make_async_copy(
+                gradient_part.at[slot, :, pl.ds(0, size)], gradient.at[:, target],
+                out_sem.at[1, slot],
+            ),
+            pltpu.make_async_copy(
+                rows_part.at[slot, pl.ds(0, size), :], gradient_rows.at[target, :],
+                out_sem.at[2, slot],
+            ),
+        ]
+        for copy in copies:
+            copy.start()
+        stores.append(copies)
+        if n + 2 < len(plan):
+            fetched.append(fetch(n + 2))
+
+    def land(zi):
+        if zi:
+            received(zz[zi])
+            share(zi, 1, zrows)
+        received(yy[zi, 1], yy[zi, 3])
+        share(zi, 1, yrows)
+        for yi in (0, 1):
             for k in KS if zi or yi else ():
-                xx[zi, yi, k].wait_recv()
-                rows = pl.ds(pl.multiple_of(GX_PART * flip(x, k), 8), GX_PART)
-                share(whole.at[block_of(zi, yi)], block_of(zi, yi), rows, every)
+                received(xx[zi, yi, k])
+                share(zi, yi, (GX_PART * flip(x, k), GX_PART))
+        received(*shared[zi])
+        landed = within(4 * flip(z, zi), (0, 4 * height))
+        copy = pltpu.make_async_copy(
+            whole.at[landed, :], whole_out.at[landed, :], whole_sem.at[zi]
+        )
+        copy.start()
+        saved.append(copy)
+
+    def relay(zi):
+        received(zyz[zi])
+        y_across(zi)
+        share(zi, 0, zyrows)
+
     keep.wait()
-    for copy in shared:
-        copy.wait_recv()
+    relay(1)
+    land(0)
+    window(0)
+    relay(3)
+    land(1)
+    window(1)
+    land(3)
+    relay(2)
+    window(2)
+    land(2)
+    window(3)
+    for copies in stores[2:]:
+        for copy in copies:
+            copy.wait()
+    for copy in saved:
+        copy.wait()
     for copy in started:
         copy.wait_send()
 
 
-def gather_blocks(mine):
+def forward_blocks(mine, tokens, shift, factor, cotangent):
     rows, features = mine.shape
-    copies = 120
-    whole = pl.pallas_call(
-        gather_kernel,
-        out_shape=jax.ShapeDtypeStruct((16, rows, features), mine.dtype),
-        in_specs=[pl.BlockSpec(memory_space=pl.ANY)],
-        out_specs=pl.BlockSpec(memory_space=pl.ANY),
+    count, units = cotangent.shape
+    copies, widest = 120, FAR * TILE
+    bf16 = jnp.bfloat16
+    vmem = pl.BlockSpec(memory_space=pltpu.VMEM)
+    anywhere = pl.BlockSpec(memory_space=pl.ANY)
+    return pl.pallas_call(
+        forward_kernel,
+        out_shape=(
+            jax.ShapeDtypeStruct((16 * rows, features), bf16),
+            jax.ShapeDtypeStruct((count, units), bf16),
+            jax.ShapeDtypeStruct((count, units), bf16),
+            jax.ShapeDtypeStruct((units, count), bf16),
+            jax.ShapeDtypeStruct((count, features), bf16),
+        ),
+        in_specs=[vmem, vmem, vmem, vmem, anywhere],
+        out_specs=(anywhere, anywhere, anywhere, anywhere, vmem),
         scratch_shapes=[
+            pltpu.VMEM((16 * rows, features), bf16),
+            pltpu.VMEM((2, count, widest), bf16),
+            pltpu.VMEM((2, count, widest), bf16),
+            pltpu.VMEM((2, count, widest), bf16),
+            pltpu.VMEM((2, widest, count), bf16),
             pltpu.SemaphoreType.DMA(()),
             pltpu.SemaphoreType.DMA((copies,)),
             pltpu.SemaphoreType.DMA((copies,)),
+            pltpu.SemaphoreType.DMA((2,)),
+            pltpu.SemaphoreType.DMA((3, 2)),
+            pltpu.SemaphoreType.DMA((4,)),
         ],
-        compiler_params=pltpu.CompilerParams(collective_id=1, has_side_effects=True),
-        name="gather_blocks",
-    )(mine)
-    return whole.reshape(16 * rows, features)
+        compiler_params=pltpu.CompilerParams(
+            collective_id=1, has_side_effects=True, vmem_limit_bytes=60 << 20
+        ),
+        name="forward_blocks",
+    )(mine, tokens, shift, factor, cotangent)
 
 
 def per_device(tokens, timesteps, table, weight_values, weight_scales, cotangent):
-    moved, factor = modulate(tokens, timesteps, table)
-    upstream = cotangent.astype(jnp.float32)
-    weight = gather_blocks(dequantize(weight_values, weight_scales))
-    preact = jnp.einsum("td,fd->tf", moved, weight, preferred_element_type=jnp.float32)
-    gelu_value, derivative = gelu_slope(preact)
-    hidden = gelu_value.astype(jnp.bfloat16)
-    grad_pre = (upstream * derivative).astype(jnp.bfloat16)
+    shift, factor = pick(timesteps, table)
+    weight, hidden, grad_pre, gradient_rows, moved = forward_blocks(
+        dequantize(weight_values, weight_scales), tokens, shift, factor, cotangent
+    )
     grad_weight, grad_tokens = reduce_blocks(
-        grad_pre, moved, weight, tokens, factor.reshape(factor.shape[0], -1)
+        gradient_rows, grad_pre, moved, weight, tokens, factor
     )
     return (hidden, grad_weight, grad_tokens)
 

time: 199 us -> 188 us (0.945); the launches traced: 199 us -> 185 us
  matrix products: 23.8 us -> 1.19 us
  Pallas kernels: 153 us -> 170 us
  other arithmetic: 8.7 us -> 2.45 us
  local copies, waits for them, and re-layouts: 13 us -> 10.9 us
    dot_general x2 -> x1, matrix products: 23.8 us -> 1.19 us  [pick(): jnp.dot(onehot, table.reshape(step_count, 2 * features), precision=lax.Pr...]
    pallas_call x1, Pallas kernels: 62 us -> 73.4 us  [forward_blocks(): pl.pallas_call(forward_kernel, out_shape=(jax.ShapeDtypeStruct((16 * rows...]
    transpose x1 -> x0, local copies, waits for them, and re-layouts: 7.56 us -> none  [reduce_blocks(): grad_pre.T.reshape(-1, OWN_ROWS, count)]
    pallas_call x1, Pallas kernels: 90.5 us -> 96.4 us  [reduce_blocks(): pl.pallas_call(reduce_kernel, out_shape=(jax.ShapeDtypeStruct((OWN_ROWS,...]
    unnamed x14 -> x12, local copies, waits for them, and re-layouts: 4.64 us -> 10.1 us
    reduce_sum x2 -> x0, other arithmetic: 4.31 us -> none  [the longest x1 2.29 us: modulate(): jnp.mean(centre * centre, axis=2, keepdims=True) + epsilon]
    convert_element_type x1 -> x0, other arithmetic: 2.46 us -> none  [modulate(): (normed * factor + picked[:, 0][:, None, :]).reshape(-1, features)]
where the time goes in v5:
time: 188 us; the launch traced here: 185 us
  Pallas kernels  170 us (90%)
  local copies, waits for them, and re-layouts  10.9 us (6%)
  other arithmetic  2.45 us (1%)
    pallas_call x1, Pallas kernels, reduce_blocks(): pl.pallas_call(reduce_kernel, out_shape=(jax.ShapeDtypeStruct((OWN_ROWS,...  96.4 us
    pallas_call x1, Pallas kernels, forward_blocks(): pl.pallas_call(forward_kernel, out_shape=(jax.ShapeDtypeStruct((16 * rows...  73.4 us
    unnamed x12, local copies, waits for them, and re-layouts  10.1 us

profile of v5, /device:TPU:0, one launch (start us, length us, event | category | flops | bytes accessed | tf_op | source)
XLA Modules:
  0.0 185.1 jit_solution(9753377248762120461)
XLA Ops:
  0.6 0.0 copy-start.3
  0.6 1.3 copy.12
  1.9 0.0 copy-start.2
  1.9 1.2 fusion.1
  3.1 0.6 slice_add_fusion
  3.7 0.0 copy-done.3
  3.7 0.1 copy.10
  3.9 0.7 mul.11
  4.6 0.0 copy-done.2
  4.6 1.8 fusion.mine
  6.4 73.4 %forward_blocks.1 = (bf16[4864,1920]{1,0:T(8,128)(2,1)}, bf16[512,4864]{1,0:T(8,128)(2,1)}, bf16[512,4864]{1,0:T(8,128)(2,1)}, bf16[4864,512]{1,0:T(8,128)(2,1)}, bf16[512,1920]{1,0:T(8,128)(2,1)}) custom-call(bf16[304,1920]{1,0:T(8,128)(2,1)} %fusion.mine, bf16[512,1920]{1,0:T(8,128)(2,1)} %tokens.3, f32[2,1920]{1,0:T(2,128)} %get-tuple-element.18.shift, ...), custom_call_target="tpu_custom_call" | custom-call | tf_op jit(solution)/shard_map/forward_blocks/pallas_call | solution.py:658
  79.8 96.4 %reduce_blocks.1 = (f32[304,1920]{1,0:T(8,128)}, bf16[512,1920]{1,0:T(8,128)(2,1)}) custom-call(bf16[16,304,512]{2,1,0:T(8,128)(2,1)} %bitcast.10, bf16[512,4864]{1,0:T(8,128)(2,1)} %get-tuple-element.12.gradient, bf16[512,1920]{1,0:T(8,128)(2,1)} %get-tuple-element.13.moved, bf16[4864,1920]{1,0:T(8,128)(2,1)} %get-tuple-element.14.weight, ...), custom_call_target="tpu_custom_call" | custom-call | tf_op jit(solution)/shard_map/reduce_blocks/pallas_call | solution.py:391
  176.2 0.0 copy-start
  176.2 5.2 %copy.17 = bf16[512,4864]{1,0:T(8,128)(2,1)} copy(bf16[512,4864]{1,0:T(8,128)(2,1)} %get-tuple-element.22) | data formatting | bytes 9961472
  181.4 0.0 copy-done
  181.4 0.0 copy-start.1
  181.4 1.4 copy.18
  182.8 1.0 copy-done.1
  183.8 1.3 copy.19
Async XLA Ops:
  0.6 3.1 %copy-start.3 = (bf16[304,15]{0,1:T(8,128)(2,1)S(1)}, bf16[304,15]{0,1:T(8,128)(2,1)}, u32[]{:S(2)}) copy-start(bf16[304,15]{0,1:T(8,128)(2,1)} %param.10) | copy-start | bytes 27364
  1.9 2.7 %copy-start.2 = (bf16[304,1920]{1,0:T(8,128)(2,1)S(1)}, bf16[304,1920]{1,0:T(8,128)(2,1)}, u32[]{:S(2)}) copy-start(bf16[304,1920]{1,0:T(8,128)(2,1)} %param.9) | copy-start | bytes 3502084
  176.2 5.2 %copy-start = (f32[304,1920]{1,0:T(8,128)S(1)}, f32[304,1920]{1,0:T(8,128)}, u32[]{:S(2)}) copy-start(f32[304,1920]{1,0:T(8,128)} %get-tuple-element.23) | copy-start | bytes 7004164
  181.4 2.4 %copy-start.1 = (bf16[512,1920]{1,0:T(8,128)(2,1)S(1)}, bf16[512,1920]{1,0:T(8,128)(2,1)}, u32[]{:S(2)}) copy-start(bf16[512,1920]{1,0:T(8,128)(2,1)} %get-tuple-element.24) | copy-start | bytes 5898244

commit v6 on v5

--- a/solution.py
+++ b/solution.py
@@ -43,7 +43,7 @@
 
 MESH = pl.DeviceIdType.MESH
 KS = (1, 3, 2)
-Z_ROWS, X_ROWS, Y_ROWS = 112, 96, 96
+Z_ROWS, X_ROWS, Y_ROWS = 96, 96, 112
 X_AT, Y_AT = Z_ROWS, Z_ROWS + X_ROWS
 OWN_ROWS = Z_ROWS + X_ROWS + Y_ROWS
 WINDOWS = ((0, 1024), (1024, 1024), (2048, 1024), (3072, 1024), (4096, 768))

time: 188 us -> 185 us (0.984); the launches traced: 185 us -> 184 us
  no operation moved by 1% of the time
where the time goes in v6:
time: 185 us; the launch traced here: 184 us
  Pallas kernels  169 us (91%)
  local copies, waits for them, and re-layouts  10.9 us (6%)
  other arithmetic  2.45 us (1%)
    pallas_call x1, Pallas kernels, reduce_blocks(): pl.pallas_call(reduce_kernel, out_shape=(jax.ShapeDtypeStruct((OWN_ROWS,...  95.9 us
    pallas_call x1, Pallas kernels, forward_blocks(): pl.pallas_call(forward_kernel, out_shape=(jax.ShapeDtypeStruct((16 * rows...  73.4 us
    unnamed x12, local copies, waits for them, and re-layouts  10.1 us

profile of v6, /device:TPU:0, one launch (start us, length us, event | category | flops | bytes accessed | tf_op | source)
XLA Modules:
  0.0 184.5 jit_solution(4037020578659343342)
XLA Ops:
  0.6 0.0 copy-start.3
  0.6 1.3 copy.12
  1.9 0.0 copy-start.2
  1.9 1.2 fusion.1
  3.1 0.6 slice_add_fusion
  3.7 0.0 copy-done.3
  3.7 0.1 copy.10
  3.9 0.7 mul.11
  4.6 0.0 copy-done.2
  4.6 1.8 fusion.mine
  6.4 73.4 %forward_blocks.1 = (bf16[4864,1920]{1,0:T(8,128)(2,1)}, bf16[512,4864]{1,0:T(8,128)(2,1)}, bf16[512,4864]{1,0:T(8,128)(2,1)}, bf16[4864,512]{1,0:T(8,128)(2,1)}, bf16[512,1920]{1,0:T(8,128)(2,1)}) custom-call(bf16[304,1920]{1,0:T(8,128)(2,1)} %fusion.mine, bf16[512,1920]{1,0:T(8,128)(2,1)} %tokens.3, f32[2,1920]{1,0:T(2,128)} %get-tuple-element.18.shift, ...), custom_call_target="tpu_custom_call" | custom-call | tf_op jit(solution)/shard_map/forward_blocks/pallas_call | solution.py:658
  79.8 95.9 %reduce_blocks.1 = (f32[304,1920]{1,0:T(8,128)}, bf16[512,1920]{1,0:T(8,128)(2,1)}) custom-call(bf16[16,304,512]{2,1,0:T(8,128)(2,1)} %bitcast.10, bf16[512,4864]{1,0:T(8,128)(2,1)} %get-tuple-element.12.gradient, bf16[512,1920]{1,0:T(8,128)(2,1)} %get-tuple-element.13.moved, bf16[4864,1920]{1,0:T(8,128)(2,1)} %get-tuple-element.14.weight, ...), custom_call_target="tpu_custom_call" | custom-call | tf_op jit(solution)/shard_map/reduce_blocks/pallas_call | solution.py:391
  175.7 0.0 copy-start
  175.7 5.2 %copy.17 = bf16[512,4864]{1,0:T(8,128)(2,1)} copy(bf16[512,4864]{1,0:T(8,128)(2,1)} %get-tuple-element.22) | data formatting | bytes 9961472
  180.8 0.0 copy-done
  180.8 0.0 copy-start.1
  180.8 1.4 copy.18
  182.2 1.0 copy-done.1
  183.2 1.3 copy.19
Async XLA Ops:
  0.6 3.1 %copy-start.3 = (bf16[304,15]{0,1:T(8,128)(2,1)S(1)}, bf16[304,15]{0,1:T(8,128)(2,1)}, u32[]{:S(2)}) copy-start(bf16[304,15]{0,1:T(8,128)(2,1)} %param.10) | copy-start | bytes 27364
  1.9 2.7 %copy-start.2 = (bf16[304,1920]{1,0:T(8,128)(2,1)S(1)}, bf16[304,1920]{1,0:T(8,128)(2,1)}, u32[]{:S(2)}) copy-start(bf16[304,1920]{1,0:T(8,128)(2,1)} %param.9) | copy-start | bytes 3502084
  175.7 5.2 %copy-start = (f32[304,1920]{1,0:T(8,128)S(1)}, f32[304,1920]{1,0:T(8,128)}, u32[]{:S(2)}) copy-start(f32[304,1920]{1,0:T(8,128)} %get-tuple-element.23) | copy-start | bytes 7004164
  180.8 2.4 %copy-start.1 = (bf16[512,1920]{1,0:T(8,128)(2,1)S(1)}, bf16[512,1920]{1,0:T(8,128)(2,1)}, u32[]{:S(2)}) copy-start(bf16[512,1920]{1,0:T(8,128)(2,1)} %get-tuple-element.24) | copy-start | bytes 5898244

commit v7 on v6

--- a/solution.py
+++ b/solution.py
@@ -237,18 +237,6 @@
             zb.at[:, :, pl.ds(quarter(flip(x, k)), 512)], zr2.at[k - 1],
             s2.at[k - 1], r2.at[k - 1], to(dx=k),
         ))
-    for copy in first["y"]:
-        copy.wait_recv()
-    for zi in (1, 3, 2, 0):
-        columns = pl.ds(half(y), 1024)
-        add_rows(
-            Y_ROWS, store_to(yb.at[zi]),
-            [shifted(own.at[zi, 0], Y_AT, columns)] + [plain(yr1.at[k - 1, zi]) for k in KS],
-        )
-        if zi:
-            second["y"].append(send(
-                yb.at[zi], yr2.at[zi - 1], s2.at[2 + zi], r2.at[2 + zi], to(dz=zi)
-            ))
     for copy in first["x"]:
         copy.wait_recv()
     for yi in (1, 0):
@@ -263,6 +251,18 @@
             second["x"].append(send(
                 xb.at[:, yi, :, pl.ds(part(flip(y, k) // 2), 256)], xr2.at[k - 1],
                 s2.at[5 + k], r2.at[5 + k], to(dy=k),
+            ))
+    for copy in first["y"]:
+        copy.wait_recv()
+    for zi in (1, 3, 2, 0):
+        columns = pl.ds(half(y), 1024)
+        add_rows(
+            Y_ROWS, store_to(yb.at[zi]),
+            [shifted(own.at[zi, 0], Y_AT, columns)] + [plain(yr1.at[k - 1, zi]) for k in KS],
+        )
+        if zi:
+            second["y"].append(send(
+                yb.at[zi], yr2.at[zi - 1], s2.at[2 + zi], r2.at[2 + zi], to(dz=zi)
             ))
 
     per_sample = count // factor.shape[0]

time: 185 us -> 185 us (level)
  no operation moved by 1% of the time
where the time goes in v7:
time: 185 us
  Pallas kernels  170 us (92%)
  local copies, waits for them, and re-layouts  10.9 us (6%)
  other arithmetic  2.45 us (1%)
    pallas_call x1, Pallas kernels, reduce_blocks(): pl.pallas_call(reduce_kernel, out_shape=(jax.ShapeDtypeStruct((OWN_ROWS,...  96.4 us
    pallas_call x1, Pallas kernels, forward_blocks(): pl.pallas_call(forward_kernel, out_shape=(jax.ShapeDtypeStruct((16 * rows...  73.4 us
    unnamed x12, local copies, waits for them, and re-layouts  10.1 us

profile of v7, /device:TPU:0, one launch (start us, length us, event | category | flops | bytes accessed | tf_op | source)
XLA Modules:
  0.0 185.1 jit_solution(2717444367917708452)
XLA Ops:
  0.6 0.0 copy-start.3
  0.6 1.3 copy.12
  1.9 0.0 copy-start.2
  1.9 1.2 fusion.1
  3.1 0.6 slice_add_fusion
  3.7 0.0 copy-done.3
  3.7 0.1 copy.10
  3.9 0.7 mul.11
  4.6 0.0 copy-done.2
  4.6 1.8 fusion.mine
  6.4 73.4 %forward_blocks.1 = (bf16[4864,1920]{1,0:T(8,128)(2,1)}, bf16[512,4864]{1,0:T(8,128)(2,1)}, bf16[512,4864]{1,0:T(8,128)(2,1)}, bf16[4864,512]{1,0:T(8,128)(2,1)}, bf16[512,1920]{1,0:T(8,128)(2,1)}) custom-call(bf16[304,1920]{1,0:T(8,128)(2,1)} %fusion.mine, bf16[512,1920]{1,0:T(8,128)(2,1)} %tokens.3, f32[2,1920]{1,0:T(2,128)} %get-tuple-element.18.shift, ...), custom_call_target="tpu_custom_call" | custom-call | tf_op jit(solution)/shard_map/forward_blocks/pallas_call | solution.py:658
  79.8 96.4 %reduce_blocks.1 = (f32[304,1920]{1,0:T(8,128)}, bf16[512,1920]{1,0:T(8,128)(2,1)}) custom-call(bf16[16,304,512]{2,1,0:T(8,128)(2,1)} %bitcast.10, bf16[512,4864]{1,0:T(8,128)(2,1)} %get-tuple-element.12.gradient, bf16[512,1920]{1,0:T(8,128)(2,1)} %get-tuple-element.13.moved, bf16[4864,1920]{1,0:T(8,128)(2,1)} %get-tuple-element.14.weight, ...), custom_call_target="tpu_custom_call" | custom-call | tf_op jit(solution)/shard_map/reduce_blocks/pallas_call | solution.py:391
  176.2 0.0 copy-start
  176.2 5.2 %copy.17 = bf16[512,4864]{1,0:T(8,128)(2,1)} copy(bf16[512,4864]{1,0:T(8,128)(2,1)} %get-tuple-element.22) | data formatting | bytes 9961472
  181.4 0.0 copy-done
  181.4 0.0 copy-start.1
  181.4 1.4 copy.18
  182.8 1.0 copy-done.1
  183.8 1.3 copy.19
Async XLA Ops:
  0.6 3.1 %copy-start.3 = (bf16[304,15]{0,1:T(8,128)(2,1)S(1)}, bf16[304,15]{0,1:T(8,128)(2,1)}, u32[]{:S(2)}) copy-start(bf16[304,15]{0,1:T(8,128)(2,1)} %param.10) | copy-start | bytes 27364
  1.9 2.7 %copy-start.2 = (bf16[304,1920]{1,0:T(8,128)(2,1)S(1)}, bf16[304,1920]{1,0:T(8,128)(2,1)}, u32[]{:S(2)}) copy-start(bf16[304,1920]{1,0:T(8,128)(2,1)} %param.9) | copy-start | bytes 3502084
  176.2 5.2 %copy-start = (f32[304,1920]{1,0:T(8,128)S(1)}, f32[304,1920]{1,0:T(8,128)}, u32[]{:S(2)}) copy-start(f32[304,1920]{1,0:T(8,128)} %get-tuple-element.23) | copy-start | bytes 7004164
  181.4 2.4 %copy-start.1 = (bf16[512,1920]{1,0:T(8,128)(2,1)S(1)}, bf16[512,1920]{1,0:T(8,128)(2,1)}, u32[]{:S(2)}) copy-start(bf16[512,1920]{1,0:T(8,128)(2,1)} %get-tuple-element.24) | copy-start | bytes 5898244
